TPU v7x, 128 devices: a whole 4x4x4 slice. The times are simulated.
128 devices in a mesh: slab: 64 (over z, y, x), sub: 2 (over core).
Axes of the slice: x: 4, y: 4, z: 4, core: 2. Of those that a mesh axis runs over, the one named last changes fastest.
Arguments:
- part_cells: int32 [128, 128, 256], P(('slab', 'sub')), may hold values from 0 to 8191
- part_offsets: float32 [128, 128, 3, 256], P(('slab', 'sub')), may hold values from 0 to 1
- part_counts: int32 [128, 128], P(('slab', 'sub')), may hold values from 32 to 256, as said below
- w_first: bfloat16 [16, 27], replicated, may hold values from -1.25 to 1.25
- w_mid: bfloat16 [16, 432], replicated, may hold values from -0.3125 to 0.3125
- w_last: bfloat16 [16, 432], replicated, may hold values from -0.3125 to 0.3125
- w_head: bfloat16 [3, 32], replicated, may hold values from -1 to 1
- cotangent: bfloat16 [3, 256, 16, 256], P(None, 'slab', 'sub'), may hold values from -6 to 6
Outputs:
- force: bfloat16 [3, 256, 16, 256], P(None, 'slab', 'sub')
- grad_first: float32 [16, 27], replicated
- grad_mid: float32 [16, 432], replicated
- grad_last: float32 [16, 432], replicated
- grad_head: float32 [3, 32], replicated
Inputs may be any that keep to these rules, and one draw needn't show every extreme that they name: part_counts[s, d] is the number of used slots among the 256 slots from device s to brick d; one brick, drawn from the seed, gets 256 from every device. part_cells[s, d, k] is the cell (i * 8 + j) * 256 + l in brick d's own cells; slots at or above part_counts[s, d] are unused.
All inputs are finite; a program needn't handle non-finite values.
Results may differ from a plain program's by a relative error of at most 0.003.
The roundings to bfloat16 on the way count: a program that leaves them out, or rounds other values in their place, can miss the bound.
Values may be sent and summed in bfloat16 or wider, within the bound.
A program may use at most 192 MiB of HBM per device.

v0:
```python
import math

import jax
import jax.numpy as jnp
from jax import lax
from jax.sharding import PartitionSpec as P


def padded_2(x, sides, width):
    for axis, dim in sides:
        devices, length = (lax.axis_size(axis), x.shape[dim])
        up = [(i, (i + 1) % devices) for i in range(devices)]
        down = [(j, i) for i, j in up]
        last = lax.slice_in_dim(x, length - width, length, axis=dim)
        initial = lax.slice_in_dim(x, 0, width, axis=dim)
        before = lax.ppermute(last, axis, up)
        after = lax.ppermute(initial, axis, down)
        x = jnp.concatenate([before, x, after], axis=dim)
    return x


def passed_along(x, axis, by):
    devices = lax.axis_size(axis)
    return lax.ppermute(x, axis, [(i, (i + by) % devices) for i in range(devices)])


def silu_slope(value):
    sigma = jax.nn.sigmoid(value)
    return sigma * (1.0 + value * (1.0 - sigma))


def z_stack(plane):
    return jnp.concatenate([jnp.roll(plane, 1, axis=2), plane, jnp.roll(plane, -1, axis=2)], 0)


def conv_planes(padded, kernel, stacker):
    chans = padded.shape[0]
    out_x = padded.shape[1] - 2
    out_y = padded.shape[2] - 2
    out_chans = kernel.shape[0]
    blocks = kernel.reshape(out_chans, 3, 3, 3 * chans)
    stacks = [stacker(padded[:, plane]) for plane in range(out_x + 2)]
    depth_z = stacks[0].shape[2]
    results = []
    for plane in range(out_x):
        total = jnp.zeros((out_chans, out_y * depth_z), jnp.float32)
        for shift_x in range(3):
            for shift_y in range(3):
                piece = stacks[plane + shift_x][:, shift_y : shift_y + out_y].reshape(
                    3 * chans, out_y * depth_z
                )
                total = total + jnp.dot(
                    blocks[:, shift_x, shift_y], piece, preferred_element_type=jnp.float32
                )
        results.append(total.reshape(out_chans, out_y, depth_z))
    return jnp.stack(results, 1)


def weight_grad(padded, grad, stacker):
    chans = padded.shape[0]
    out_x = grad.shape[1]
    out_y = grad.shape[2]
    depth_z = grad.shape[3]
    out_chans = grad.shape[0]
    totals = [
        [jnp.zeros((out_chans, 3 * chans), jnp.float32) for shift_y in range(3)]
        for shift_x in range(3)
    ]
    for plane in range(out_x):
        grad_plane = grad[:, plane].reshape(out_chans, out_y * depth_z)
        for shift_x in range(3):
            stacked = stacker(padded[:, plane + shift_x])
            for shift_y in range(3):
                piece = stacked[:, shift_y : shift_y + out_y].reshape(3 * chans, out_y * depth_z)
                totals[shift_x][shift_y] = totals[shift_x][shift_y] + lax.dot_general(
                    grad_plane, piece, (((1,), (1,)), ((), ())), preferred_element_type=jnp.float32
                )
    joined = jnp.stack([jnp.stack(totals[shift_x], axis=1) for shift_x in range(3)], axis=1)
    return joined.reshape(out_chans, 27 * chans)


def flip_kernel(weights, chans):
    out_chans = weights.shape[0]
    shaped = weights.reshape(out_chans, 3, 3, 3, chans)[:, ::-1, ::-1, ::-1, :]
    return shaped.transpose(4, 1, 2, 3, 0).reshape(chans, 27 * out_chans)


def with_rims(field):
    return padded_2(field, (("slab", 1), ("sub", 2)), 1)


def finish(
    density_rim,
    pre_one,
    hidden_one,
    hidden_one_rim,
    pre_two,
    hidden_two_rim,
    w_mid,
    w_last,
    w_head,
    ct_field,
    rims,
    stacker,
):
    channels = w_mid.shape[0]
    extent = pre_one.shape[1:]
    pre_three = conv_planes(hidden_two_rim, w_last, stacker)
    hidden_three = jax.nn.silu(pre_three).astype(jnp.bfloat16)
    features = jnp.concatenate([hidden_three, hidden_one], 0).reshape(2 * channels, -1)
    ct_flat = ct_field.reshape(3, -1)
    force = jnp.dot(w_head, features, preferred_element_type=jnp.float32).astype(jnp.bfloat16)
    force = force.reshape((3,) + extent)
    grad_head = lax.dot_general(
        ct_flat, features, (((1,), (1,)), ((), ())), preferred_element_type=jnp.float32
    )
    back_features = jnp.dot(w_head.T, ct_flat, preferred_element_type=jnp.float32)
    grad_three = (back_features[:channels] * silu_slope(pre_three.reshape(channels, -1))).astype(
        jnp.bfloat16
    )
    grad_three = grad_three.reshape((channels,) + extent)
    grad_last = weight_grad(hidden_two_rim, grad_three, stacker)
    back_two = conv_planes(rims(grad_three), flip_kernel(w_last, channels), stacker)
    grad_two = (back_two * silu_slope(pre_two)).astype(jnp.bfloat16)
    grad_mid = weight_grad(hidden_one_rim, grad_two, stacker)
    back_one = conv_planes(rims(grad_two), flip_kernel(w_mid, channels), stacker)
    back_one = back_one + back_features[channels:].reshape((channels,) + extent)
    grad_one = (back_one * silu_slope(pre_one)).astype(jnp.bfloat16)
    grad_first = weight_grad(density_rim, grad_one, stacker)
    return (force, grad_first, grad_mid, grad_last, grad_head)


def per_device(part_cells, part_offsets, part_counts, w_first, w_mid, w_last, w_head, cotangent):
    n_slab = lax.axis_size("slab")
    n_sub = lax.axis_size("sub")
    width_x = cotangent.shape[1]
    width_y = cotangent.shape[2]
    depth_z = cotangent.shape[3]
    slot_cap = part_cells.shape[2]
    got_cells, got_offsets, got_counts = (
        lax.all_to_all(part_cells, ("slab", "sub"), split_axis=1, concat_axis=0, tiled=True),
        lax.all_to_all(part_offsets, ("slab", "sub"), split_axis=1, concat_axis=0, tiled=True),
        lax.all_to_all(part_counts, ("slab", "sub"), split_axis=1, concat_axis=0, tiled=True),
    )
    slot_cells = got_cells.reshape(-1, slot_cap)
    offsets = got_offsets.reshape(-1, 3, slot_cap)
    counts = got_counts.reshape(-1)
    slot_ids = jnp.arange(slot_cap, dtype=jnp.int32)
    live = (slot_ids[None, :] < counts[:, None]).astype(jnp.float32)
    cell_x = slot_cells // (width_y * depth_z)
    cell_y = slot_cells // depth_z % width_y
    cell_z = slot_cells % depth_z
    frac_x = offsets[:, 0]
    frac_y = offsets[:, 1]
    frac_z = offsets[:, 2]
    padded = jnp.zeros(((width_x + 1) * (width_y + 1) * depth_z,), jnp.float32)
    for corner_x in (0, 1):
        weight_x = frac_x if corner_x else 1.0 - frac_x
        for corner_y in (0, 1):
            weight_y = frac_y if corner_y else 1.0 - frac_y
            for corner_z in (0, 1):
                weight_z = frac_z if corner_z else 1.0 - frac_z
                share = live * weight_x * weight_y * weight_z
                index = ((cell_x + corner_x) * (width_y + 1) + cell_y + corner_y) * depth_z + (
                    cell_z + corner_z
                ) % depth_z
                padded = padded.at[index.reshape(-1)].add(share.reshape(-1))
    padded = padded.reshape(width_x + 1, width_y + 1, depth_z)
    from_below = passed_along(padded[width_x], "slab", 1)
    core = padded[:width_x].at[0].add(from_below)
    from_side = passed_along(core[:, width_y], "sub", 1)
    density = core[:, :width_y].at[:, 0].add(from_side)
    density_b = density.astype(jnp.bfloat16)[None]
    density_rim = with_rims(density_b)
    pre_one = conv_planes(density_rim, w_first, z_stack)
    hidden_one = jax.nn.silu(pre_one).astype(jnp.bfloat16)
    hidden_one_rim = with_rims(hidden_one)
    pre_two = conv_planes(hidden_one_rim, w_mid, z_stack)
    hidden_two = jax.nn.silu(pre_two).astype(jnp.bfloat16)
    hidden_two_rim = with_rims(hidden_two)
    force, grad_first, grad_mid, grad_last, grad_head = finish(
        density_rim,
        pre_one,
        hidden_one,
        hidden_one_rim,
        pre_two,
        hidden_two_rim,
        w_mid,
        w_last,
        w_head,
        cotangent,
        with_rims,
        z_stack,
    )
    sum_first, sum_mid, sum_last, sum_head = lax.psum(
        (grad_first, grad_mid, grad_last, grad_head), ("slab", "sub")
    )
    loss_scale = 1.0 / math.sqrt(width_x * n_slab * width_y * n_sub * depth_z)
    return (
        force,
        loss_scale * sum_first,
        loss_scale * sum_mid,
        loss_scale * sum_last,
        loss_scale * sum_head,
    )


def solution(mesh):
    in_specs = (
        P(("slab", "sub"), None, None),
        P(("slab", "sub"), None, None, None),
        P(("slab", "sub"), None),
        P(),
        P(),
        P(),
        P(),
        P(None, "slab", "sub", None),
    )
    out_specs = (P(None, "slab", "sub", None), P(), P(), P(), P())
    return jax.shard_map(
        per_device, mesh=mesh, in_specs=in_specs, out_specs=out_specs, check_vma=False
    )
```

profile of v0, /device:TPU:1, one launch (start us, length us, event | category | flops | bytes accessed | tf_op | source)
XLA Modules:
  0.0 1670.1 jit_solution(12769515616592546914)
XLA Ops:
  0.6 1.4 copy.241
  2.0 11.5 all-to-all-start.1
  13.5 1.7 copy.240
  15.2 2.1 copy.242
  17.3 5.9 all-to-all-done.1
  23.1 4.5 all-to-all-start
  27.6 2.4 reduce.4
  30.1 7.5 all-to-all-done
  37.7 4.2 all-to-all-start.2
  41.9 3.0 compare_select_fusion
  44.9 1.8 compare_select_fusion.1
  46.6 1.3 compare_select_fusion.5
  47.9 7.6 all-to-all-done.2
  55.9 0.9 fusion.42
  56.8 171.0 %scatter_custom_fusion = f32[11520]{0:T(1024)S(1)} fusion(s32[32768]{0:T(1024)S(1)} %bitcast.1767, f32[32768]{0:T(1024)S(1)} %get-tuple-element.95, f32[]{:T(128)} %constant.137.clone.1), kind=kCustom, calls=%fused_computation.492 | custom fusion | flops 32768 | bytes 46084 | tf_op jit(solution)/shard_map/scatter-add | solution.py:167
  227.8 174.7 %scatter_fusion = f32[11520]{0:T(1024)S(1)} fusion(f32[11520]{0:T(1024)S(1)} %scatter_custom_fusion, s32[32768]{0:T(1024)S(1)} %bitcast.1646, f32[32768]{0:T(1024)S(1)} %get-tuple-element.94), kind=kCustom, calls=%fused_computation.1 | custom fusion | flops 32768 | bytes 524288 | tf_op jit(solution)/shard_map/scatter-add | solution.py:167
  402.5 174.9 %scatter_fusion.1 = f32[11520]{0:T(1024)S(1)} fusion(f32[11520]{0:T(1024)S(1)} %scatter_fusion, s32[32768]{0:T(1024)S(1)} %bitcast.1645, f32[32768]{0:T(1024)S(1)} %get-tuple-element.89), kind=kCustom, calls=%fused_computation.2 | custom fusion | flops 32768 | bytes 524288 | tf_op jit(solution)/shard_map/scatter-add | solution.py:167
  577.4 174.7 %scatter_fusion.2 = f32[11520]{0:T(1024)S(1)} fusion(f32[11520]{0:T(1024)S(1)} %scatter_fusion.1, s32[32768]{0:T(1024)S(1)} %bitcast.1643, f32[32768]{0:T(1024)S(1)} %copy-done.25), kind=kCustom, calls=%fused_computation.3 | custom fusion | flops 32768 | bytes 524288 | tf_op jit(solution)/shard_map/scatter-add | solution.py:167
  752.2 174.7 %scatter_fusion.3 = f32[11520]{0:T(1024)S(1)} fusion(f32[11520]{0:T(1024)S(1)} %scatter_fusion.2, s32[32768]{0:T(1024)S(1)} %bitcast.1644, f32[32768]{0:T(1024)S(1)} %copy-done.24), kind=kCustom, calls=%fused_computation.4 | custom fusion | flops 32768 | bytes 524288 | tf_op jit(solution)/shard_map/scatter-add | solution.py:167
  926.9 174.7 %scatter_fusion.4 = f32[11520]{0:T(1024)S(1)} fusion(f32[11520]{0:T(1024)S(1)} %scatter_fusion.3, s32[32768]{0:T(1024)S(1)} %bitcast.1642, f32[32768]{0:T(1024)S(1)} %copy-done.23), kind=kCustom, calls=%fused_computation.5 | custom fusion | flops 32768 | bytes 524288 | tf_op jit(solution)/shard_map/scatter-add | solution.py:167
  1101.7 174.7 %scatter_fusion.5 = f32[11520]{0:T(1024)S(1)} fusion(f32[11520]{0:T(1024)S(1)} %scatter_fusion.4, s32[32768]{0:T(1024)S(1)} %bitcast.1641, f32[32768]{0:T(1024)S(1)} %copy-done.22), kind=kCustom, calls=%fused_computation.6 | custom fusion | flops 32768 | bytes 524288 | tf_op jit(solution)/shard_map/scatter-add | solution.py:167
  1276.4 174.7 %scatter_fusion.6 = f32[11520]{0:T(1024)S(1)} fusion(f32[11520]{0:T(1024)S(1)} %scatter_fusion.5, s32[32768]{0:T(1024)S(1)} %bitcast.1640, f32[32768]{0:T(1024)S(1)} %copy-done.21), kind=kCustom, calls=%fused_computation.7 | custom fusion | flops 32768 | bytes 524288 | tf_op jit(solution)/shard_map/scatter-add | solution.py:167
  1451.3 8.0 collective-permute-done
  1459.3 2.1 collective-permute-start.1
  1461.4 0.8 collective-permute-done.1
  1462.4 6.9 collective-permute-start.3
  1469.2 1.0 collective-permute-done.2
  1470.2 1.6 collective-permute-start.4
  1472.6 0.7 collective-permute-done.5
  1483.7 7.2 collective-permute-start.7
  1491.0 1.3 fusion.221
  1492.4 0.9 collective-permute-done.6
  1493.3 0.7 collective-permute-start.8
  1504.7 0.8 copy-done.2
  1506.3 7.0 collective-permute-start.11
  1513.9 0.8 reshape.1248
  1514.7 0.8 reshape.1229
  1515.5 0.7 copy.356
  1516.2 0.7 copy.355
  1516.9 0.7 copy.354
  1517.6 0.7 copy.353
  1518.3 0.7 copy.352
  1520.2 1.8 rev.7
  1522.0 1.8 copy.302
  1523.8 1.0 reshape_reshape.7
  1524.8 1.8 rev.6
  1526.6 1.8 copy.296
  1528.4 1.0 reshape_reshape.6
  1529.5 0.8 pad_maximum_fusion.11
  1530.3 0.7 collective-permute-start.12
  1532.4 1.0 pad_maximum_fusion.2
  1543.1 1.0 copy-done.1
  1546.0 1.6 collective-permute-start.15
  1552.9 3.6 collective-permute-done.14
  1556.5 0.8 fusion.150
  1557.3 1.6 collective-permute-start.16
  1559.8 1.0 copy.473
  1560.9 1.5 pad_maximum_fusion
  1572.8 0.7 copy-done.6
  1575.0 2.5 collective-permute-start.19
  1582.4 3.7 collective-permute-done.18
  1586.1 2.0 collective-permute-start.20
  1604.4 62.7 %all-reduce = (f32[16,27]{0,1:T(8,128)S(1)}, f32[16,432]{1,0:T(8,128)S(1)}, f32[16,432]{1,0:T(8,128)S(1)}, f32[3,32]{1,0:T(4,128)S(1)}) all-reduce(f32[16,27]{0,1:T(8,128)S(1)} %reshape.1267, f32[16,432]{1,0:T(8,128)S(1)} %reshape.1268, f32[16,432]{1,0:T(8,128)S(1)} %reshape.1269, ...), channel_id=1, replica_groups=mesh['slab'=64,'sub'=2] {'slab','sub'}, use_global_device_ids=true, to_apply=%region_8.9 | all-reduce | flops 14352 | bytes 114816 | tf_op jit(solution)/shard_map/psum | solution.py:195
  1667.1 0.7 copy.336
  (802 shorter events, 76.9 us)
Async XLA Ops:
  0.6 1490.3 %copy-start = (bf16[3,32]{1,0:T(4,128)(2,1)S(1)}, bf16[3,32]{1,0:T(4,128)(2,1)}, u32[]{:S(2)}) copy-start(bf16[3,32]{1,0:T(4,128)(2,1)} %param.18) | copy-start | bytes 580
  2.0 21.1 %all-to-all-start.1 = ((s32[1,128,1]{2,0,1:T(1,128)}), s32[1,128,1]{2,0,1:T(1,128)S(1)}, u32[]{:S(2)}, u32[]{:S(2)}) async-start(s32[1,128,1]{2,0,1:T(1,128)} %copy.241), calls=%async_computation.1 | async-start | bytes 131072 | tf_op jit(solution)/shard_map/all_to_all | solution.py:143
  23.1 14.5 all-to-all-start
  37.7 17.9 %all-to-all-start.2 = ((f32[1,128,3,256]{3,2,0,1:T(4,128)}), f32[1,128,3,256]{3,2,0,1:T(4,128)S(1)}, u32[]{:S(2)}, u32[]{:S(2)}) async-start(f32[1,128,3,256]{3,2,0,1:T(4,128)} %copy.242), calls=%async_computation.2 | async-start | bytes 1048576 | tf_op jit(solution)/shard_map/all_to_all | solution.py:142
  402.5 174.9 %copy-start.20 = (s32[32768,1]{0,1:T(1,128)S(1)}, s32[32768,1]{0,1:T(1,128)}, u32[]{:S(2)}) copy-start(s32[32768,1]{0,1:T(1,128)} %get-tuple-element.367) | copy-start | bytes 393220
  402.5 174.9 %copy-start.25 = (f32[32768]{0:T(1024)S(1)}, f32[32768]{0:T(1024)}, u32[]{:S(2)}) copy-start(f32[32768]{0:T(1024)} %get-tuple-element.93) | copy-start | bytes 393220
  577.4 174.7 %copy-start.24 = (f32[32768]{0:T(1024)S(1)}, f32[32768]{0:T(1024)}, u32[]{:S(2)}) copy-start(f32[32768]{0:T(1024)} %get-tuple-element.90) | copy-start | bytes 393220
  577.4 174.7 %copy-start.26 = (s32[32768,1]{0,1:T(1,128)S(1)}, s32[32768,1]{0,1:T(1,128)}, u32[]{:S(2)}) copy-start(s32[32768,1]{0,1:T(1,128)} %get-tuple-element.219) | copy-start | bytes 393220
  752.2 174.7 %copy-start.19 = (s32[32768,1]{0,1:T(1,128)S(1)}, s32[32768,1]{0,1:T(1,128)}, u32[]{:S(2)}) copy-start(s32[32768,1]{0,1:T(1,128)} %get-tuple-element.218) | copy-start | bytes 393220
  752.2 174.7 %copy-start.23 = (f32[32768]{0:T(1024)S(1)}, f32[32768]{0:T(1024)}, u32[]{:S(2)}) copy-start(f32[32768]{0:T(1024)} %get-tuple-element.92) | copy-start | bytes 393220
  926.9 174.7 %copy-start.18 = (s32[32768,1]{0,1:T(1,128)S(1)}, s32[32768,1]{0,1:T(1,128)}, u32[]{:S(2)}) copy-start(s32[32768,1]{0,1:T(1,128)} %get-tuple-element.54) | copy-start | bytes 393220
  926.9 174.7 %copy-start.22 = (f32[32768]{0:T(1024)S(1)}, f32[32768]{0:T(1024)}, u32[]{:S(2)}) copy-start(f32[32768]{0:T(1024)} %get-tuple-element.91) | copy-start | bytes 393220
  1101.7 174.7 %copy-start.17 = (s32[32768,1]{0,1:T(1,128)S(1)}, s32[32768,1]{0,1:T(1,128)}, u32[]{:S(2)}) copy-start(s32[32768,1]{0,1:T(1,128)} %get-tuple-element.48) | copy-start | bytes 393220
  1101.7 174.7 %copy-start.21 = (f32[32768]{0:T(1024)S(1)}, f32[32768]{0:T(1024)}, u32[]{:S(2)}) copy-start(f32[32768]{0:T(1024)} %get-tuple-element.88) | copy-start | bytes 393220
  1276.4 195.9 %copy-start.69 = (bf16[16,27]{1,0:T(8,128)(2,1)S(1)}, bf16[16,27]{1,0:T(8,128)(2,1)}, u32[]{:S(2)}) copy-start(bf16[16,27]{1,0:T(8,128)(2,1)} %param.15) | copy-start | bytes 2596
  1276.4 196.0 %copy-start.67 = (bf16[3,4,8,256]{3,2,1,0:T(8,128)(2,1)S(1)}, bf16[3,4,8,256]{3,2,1,0:T(8,128)(2,1)}, u32[]{:S(2)}) copy-start(bf16[3,4,8,256]{3,2,1,0:T(8,128)(2,1)} %param.19) | copy-start | bytes 147460
  1451.2 8.1 collective-permute-start
  1459.3 2.9 collective-permute-start.1
  1462.3 8.0 collective-permute-start.2
  1462.4 7.9 collective-permute-start.3
  1470.2 2.4 collective-permute-start.4
  1471.8 1.6 collective-permute-start.5
  1474.4 8.5 copy-start.51
  1474.5 8.3 copy-start.53
  1474.5 8.1 copy-start.55
  1474.6 7.7 copy-start.37
  1474.6 7.5 copy-start.39
  1474.7 7.2 copy-start.41
  1474.8 6.7 copy-start.27
  1474.8 5.3 copy-start.33
  1475.0 5.0 copy-start.29
  1475.0 4.7 copy-start.31
  1475.0 3.2 copy-start.35
  1475.1 2.9 copy-start.43
  1475.1 2.6 copy-start.45
  1475.2 2.1 copy-start.47
  1483.4 8.9 copy-start.63
  1483.6 10.7 copy-start.65
  1483.6 9.6 collective-permute-start.6
  1483.7 9.5 collective-permute-start.7
  1493.3 1.6 collective-permute-start.8
  1494.0 1.2 collective-permute-start.9
  1504.5 9.4 copy-start.64
  1504.5 10.2 copy-start.66
  1506.3 23.2 %collective-permute-start.10 = (bf16[16,1,8,256]{3,0,2,1:T(8,128)(2,1)}, bf16[16,1,8,256]{3,0,2,1:T(8,128)(2,1)}, u32[]{:S(2)}, u32[]{:S(2)}) collective-permute-start(bf16[16,1,8,256]{3,0,2,1:T(8,128)(2,1)} %get-tuple-element.134), channel_id=1, source_target_pairs={{0,2},{2,4},{4,6},{6,8},{8,10},{10,12},{12,14},{14,16},{16,18},{18... | collective-permute-start | bytes 196616 | tf_op jit(solution)/shard_map/ppermute | solution.py:16
  1506.3 23.2 %collective-permute-start.11 = (bf16[16,1,8,256]{3,0,2,1:T(8,128)(2,1)}, bf16[16,1,8,256]{3,0,2,1:T(8,128)(2,1)}, u32[]{:S(2)}, u32[]{:S(2)}) collective-permute-start(bf16[16,1,8,256]{3,0,2,1:T(8,128)(2,1)} %get-tuple-element.135), channel_id=1, source_target_pairs={{2,0},{4,2},{6,4},{8,6},{10,8},{12,10},{14,12},{16,14},{18,16},{20... | collective-permute-start | bytes 196616 | tf_op jit(solution)/shard_map/ppermute | solution.py:17
  1530.3 1.6 collective-permute-start.12
  1531.0 1.4 collective-permute-start.13
  1544.6 3.0 copy-start.68
  1546.0 10.5 collective-permute-start.15
  1547.9 8.6 collective-permute-start.14
  1557.3 3.5 collective-permute-start.16
  1558.9 2.0 collective-permute-start.17
  1575.0 7.4 collective-permute-start.19
  1577.4 8.6 collective-permute-start.18
  1586.1 2.9 collective-permute-start.20
  1588.1 1.5 collective-permute-start.21
  1599.2 2.2 copy-start.42
  1599.2 2.6 copy-start.56
  1599.6 2.6 copy-start.28
  1599.8 2.5 copy-start.40
  1600.5 2.5 copy-start.54
  1600.9 3.0 copy-start.38
  1601.2 3.0 copy-start.52
  (31 other events, 36.9 us)
where the time goes:
time: 1680 us; the launch traced here: 1670 us
  other arithmetic  1410 us (84%)
  blocking collectives  62.7 us (4%)
  starting transfers between devices  55.7 us (3%)
  matrix products  48.5 us (3%)
  waiting for transfers between devices  42.6 us (3%)
  local copies, waits for them, and re-layouts  42.4 us (3%)
    scatter-add x8, other arithmetic, per_device(): padded = padded.at[index.reshape(-1)].add(share.reshape(-1))  1390 us
    psum x1, blocking collectives, per_device(): lax.psum((grad_first, grad_mid, grad_last, grad_head), ('slab', 'sub'))  62.7 us
  transfers between devices with their start and end apart: 25, of which 17 were waited for; matrix products, arithmetic and copies ran while one was open for 3% of the time, Pallas kernels for 0%

commit v1 on v0

v1 whole, which is shorter than its diff:
```python
import functools
import math

import jax
import jax.numpy as jnp
from jax import lax
from jax.experimental import pallas as pl
from jax.experimental.pallas import tpu as pltpu
from jax.sharding import PartitionSpec as P

MESH = pl.DeviceIdType.MESH
F32 = jnp.float32
BF16 = jnp.bfloat16

BX, BY, NZ, CH = 4, 8, 256, 16
COLS = (BX + 2) * CH
CORE = slice(CH, CH + BX * CH)
GROUP = 4
X_ROW = (0, 8, 24, 32, 40)


def lane_roll(value, shift):
    return pltpu.roll(value, shift % value.shape[1], 1)


def dot(a, b):
    return jnp.dot(a, b, preferred_element_type=F32)


def dot_nt(a, b):
    return lax.dot_general(a, b, (((1,), (1,)), ((), ())), preferred_element_type=F32)


def join_z(stacked):
    rows = stacked.shape[0] // 3
    below = lane_roll(stacked[:rows], 1)
    above = lane_roll(stacked[2 * rows :], -1)
    return stacked[rows : 2 * rows] + below + above


def spread_z(grad):
    return jnp.concatenate([lane_roll(grad, -1), grad, lane_roll(grad, 1)], 0).astype(BF16)


def sigmoid(value):
    return 1.0 / (1.0 + jnp.exp(-value))


def slope(value):
    s = sigmoid(value)
    return s * (1.0 + value * (1.0 - s))


def source_terms(tile, half):
    cell = tile.astype(jnp.int32)
    where_z = jnp.where(cell < 0, -1, cell & 255).astype(F32)
    plane = lax.shift_right_arithmetic(cell, 8)

    def spread(value, row, rows=8):
        return jnp.broadcast_to(value[row : row + 1], (rows, 128))

    z_at = spread(where_z, half, NZ).astype(BF16)
    lanes_z = lax.broadcasted_iota(jnp.int32, (NZ, 128), 0).astype(F32).astype(BF16)
    hot = jnp.where(lanes_z == z_at, jnp.ones((), BF16), jnp.zeros((), BF16))
    at = spread(plane, half)
    at_x = lax.shift_right_arithmetic(at, 3)
    at_y = at & 7
    f = spread(tile, 2 + half)
    g = spread(tile, 4 + half)
    h = spread(tile, 6 + half)
    row = lax.broadcasted_iota(jnp.int32, (8, 128), 0)
    zero = jnp.zeros((8, 128), F32)
    weight_y = jnp.where(row == at_y, 1.0 - g, jnp.where(row == at_y + 1, g, zero))
    last_y = jnp.where(at_y == BY - 1, g, zero)
    weight_x = jnp.where(row == at_x, 1.0 - f, jnp.where(row == at_x + 1, f, zero))
    planes = []
    for i in range(BX + 1):
        here = jnp.where(at_x == i, 1.0 - f, jnp.where(at_x == i - 1, f, zero))
        planes.append(here * weight_y)
    planes.insert(2, weight_x * last_y)
    both = jnp.concatenate(planes, 0)
    tall = jnp.broadcast_to(h[:1], (48, 128))
    upper = both * tall
    lower = both - upper
    joint = jnp.concatenate([lower, upper], 0)
    high = joint.astype(BF16)
    low = (joint - high.astype(F32)).astype(BF16)
    return hot, jnp.concatenate([high, low], 0)


def body(
    got, ct, w_one, w_mid, w_last, w_mid_t, w_last_t, w_head, w_head_t,
    force, pay,
    hot_s, wt_s, dep, dep_in, dens_f, dens, one, two, g_three, g_two, pre_one, pre_two, acc,
    send, recv, send_d, recv_d,
):
    n_slab, n_sub = lax.axis_size("slab"), lax.axis_size("sub")
    slab, sub = lax.axis_index("slab"), lax.axis_index("sub")
    up, down, other = (slab + 1) % n_slab, (slab + n_slab - 1) % n_slab, (sub + 1) % n_sub
    neighbours = ((up, sub), (down, sub), (slab, other), (up, other), (down, other))
    barrier = pltpu.get_barrier_semaphore()
    for device in neighbours:
        pl.semaphore_signal(barrier, inc=1, device_id=device, device_id_type=MESH)

    dep2 = jnp.zeros((96, NZ), F32)
    sources = got.shape[0]

    def gather(step, total):
        for part in range(2):
            for k in range(GROUP):
                tile = got[step * 2 * GROUP + part * GROUP + k]
                for half in range(2):
                    hot, weights = source_terms(tile, half)
                    at = k * 256 + half * 128
                    hot_s[part, :, at : at + 128] = hot
                    wt_s[part, :, at : at + 128] = weights
            result = dot_nt(wt_s[part], hot_s[part])
            total = total + result[:96] + result[96:]
        return total

    dep2 = lax.fori_loop(0, sources // (2 * GROUP), gather, dep2)
    dep[...] = dep2[:48] + lane_roll(dep2[48:], 1)

    pl.semaphore_wait(barrier, len(neighbours))

    def remote(src, dst, at, device, sends, recvs):
        return pltpu.make_async_remote_copy(
            src_ref=src, dst_ref=dst, send_sem=sends.at[at], recv_sem=recvs.at[at],
            device_id=device, device_id_type=MESH,
        )

    upper_rows, lower_rows = pl.ds(16, 32), pl.ds(0, 24)
    copies = []
    for at, (device, rows) in enumerate(
        zip(neighbours, (upper_rows, lower_rows, pl.ds(0, 48), upper_rows, lower_rows))
    ):
        copies.append(remote(dep.at[rows], dep_in.at[at, rows], at, device, send_d, recv_d))
    for copy in copies:
        copy.start()

    dens_f[...] = jnp.zeros_like(dens_f)

    def place(source, source_x, x):
        base = (x + 2) * 16
        dens_f[base + 2 : base + 10] += source[X_ROW[source_x] : X_ROW[source_x] + 8]
        dens_f[base + 10 : base + 11] += source[16 + source_x : 17 + source_x]

    def place_other(source, source_x, x):
        base, row = (x + 2) * 16, X_ROW[source_x]
        dens_f[base : base + 2] += source[row + 6 : row + 8]
        dens_f[base + 2 : base + 3] += source[16 + source_x : 17 + source_x]
        dens_f[base + 10 : base + 12] += source[row : row + 2]

    for x in range(BX + 1):
        place(dep, x, x)
    for copy in copies:
        copy.wait()
    for x in (2, 3, 4):
        place(dep_in.at[0], x, x - 4)
    for x in (0, 1):
        place(dep_in.at[1], x, x + 4)
    for x in range(BX + 1):
        place_other(dep_in.at[2], x, x)
    for x in (2, 3, 4):
        place_other(dep_in.at[3], x, x - 4)
    for x in (0, 1):
        place_other(dep_in.at[4], x, x + 4)
    dens[...] = dens_f[...].astype(BF16)

    for y in range(BY + 2):
        taps = lane_roll(w_one[...], y).astype(BF16)
        pre = join_z(dot(taps, dens[...]))
        one[y] = (pre * sigmoid(pre)).astype(BF16)
        if 1 <= y <= BY:
            pre_one[y - 1] = pre[CORE]

    def rims(field, base):
        right, left = pl.ds(BX * CH, CH), pl.ds(CH, CH)
        before, after = pl.ds(0, CH), pl.ds((BX + 1) * CH, CH)
        core, ys = pl.ds(CH, BX * CH), pl.ds(1, BY)
        plan = (
            ((up, sub), (ys, right), (ys, before)),
            ((down, sub), (ys, left), (ys, after)),
            ((slab, other), (1, core), (BY + 1, core)),
            ((slab, other), (BY, core), (0, core)),
            ((up, other), (1, right), (BY + 1, before)),
            ((up, other), (BY, right), (0, before)),
            ((down, other), (1, left), (BY + 1, after)),
            ((down, other), (BY, left), (0, after)),
        )
        started = []
        for at, (device, src, dst) in enumerate(plan):
            copy = remote(field.at[src], field.at[dst], base + at, device, send, recv)
            copy.start()
            started.append(copy)
        return started

    def planes(field, y):
        return field[y : y + 3].reshape(3 * COLS, NZ)

    def conv(taps, field, y):
        return join_z(dot(taps[...], planes(field, y)))

    for y in range(BY):
        pre = conv(w_mid, one, y)
        pre_two[y] = pre
        two[y + 1, CORE] = (pre * sigmoid(pre)).astype(BF16)
    for copy in rims(two, 0):
        copy.wait()

    heads = []
    for y in range(BY):
        pre = conv(w_last, two, y)
        s = sigmoid(pre)
        features = jnp.concatenate([(pre * s).astype(BF16), one[y + 1, CORE]], 0)
        force[y] = dot(w_head[...], features).astype(BF16)
        heads.append((ct[y], features))
        back = dot(w_head_t[: BX * CH], ct[y])
        g_three[y + 1, CORE] = (back * (s * (1.0 + pre * (1.0 - s)))).astype(BF16)
    started = rims(g_three, 8)
    head = dot_nt(*heads[0])
    for pair in heads[1:]:
        head = head + dot_nt(*pair)

    def weight_grad(grads, field, shift):
        acc[:, 3 * COLS :] = jnp.zeros((192, 96), F32)
        for y in range(BY):
            term = dot_nt(spread_z(grads[y + 1, CORE].astype(F32)), planes(field, y))
            if y == 0:
                acc[:, : 3 * COLS] = term
            else:
                acc[:, : 3 * COLS] += term
        rows = []
        for dz in range(3):
            total = jnp.zeros((CH, 384), F32)
            for x in range(BX):
                at = (dz * BX + x) * CH
                total = total + lane_roll(acc[at : at + CH], -CH * x)
            rows.append(total)
        joint = jnp.concatenate(rows, 0)
        lane = lax.broadcasted_iota(jnp.int32, joint.shape, 1)
        joint = jnp.where((lane % 96 < 48) & (lane < 3 * COLS), joint, 0.0)
        return lane_roll(joint, shift) if shift else joint

    sums = weight_grad(g_three, two, 48)
    for copy in started:
        copy.wait()

    for y in range(BY):
        back = conv(w_last_t, g_three, y)
        g_two[y + 1, CORE] = (back * slope(pre_two[y])).astype(BF16)
    started = rims(g_two, 16)
    sums = sums + weight_grad(g_two, one, 0)
    for copy in started:
        copy.wait()

    first = jnp.zeros((192, 128), F32)
    for y in range(BY):
        back = conv(w_mid_t, g_two, y) + dot(w_head_t[BX * CH :], ct[y])
        grad = (back * slope(pre_one[y])).astype(BF16).astype(F32)
        first = first + lane_roll(dot_nt(spread_z(grad), dens[...]), -y)
    rows = []
    for dz in range(3):
        total = jnp.zeros((CH, 128), F32)
        for x in range(BX):
            at = (dz * BX + x) * CH
            total = total + lane_roll(first[at : at + CH], -(16 * x + 17))
        rows.append(total)
    joint = jnp.concatenate(rows, 0)
    lane = lax.broadcasted_iota(jnp.int32, joint.shape, 1)
    joint = jnp.where((lane % 16 < 3) & (lane < 48), joint, 0.0)
    extra = lane_roll(joint, 32)
    lane = lax.broadcasted_iota(jnp.int32, (16, 128), 1)
    row = lax.broadcasted_iota(jnp.int32, (16, 128), 0)
    total = jnp.zeros((16, 128), F32)
    for x in range(BX):
        mine = (row % BX == x) & (lane % 64 < CH)
        total = total + jnp.where(mine, lane_roll(head, -CH * x), 0.0)
    total = jnp.where(lane < CH, total, 0.0) + jnp.where(
        (lane >= CH) & (lane < 2 * CH), lane_roll(total, -48), 0.0
    )
    total = lane_roll(total, 80)
    pay[...] = sums
    pay[:, 256:384] += extra
    pay[:16, 256:384] += total


def wide_taps(weights):
    shaped = weights.reshape(CH, 3, 3, 3, CH).transpose(3, 0, 2, 1, 4)
    rows = [jnp.pad(shaped, ((0, 0), (0, 0), (0, 0), (x, BX - 1 - x), (0, 0))) for x in range(BX)]
    return jnp.stack(rows, 1).reshape(3 * BX * CH, 3 * COLS)


def flipped(weights):
    shaped = weights.reshape(CH, 3, 3, 3, CH)[:, ::-1, ::-1, ::-1]
    return shaped.transpose(4, 1, 2, 3, 0).reshape(CH, 27 * CH)


def first_taps(weights):
    width = BX + 2
    shaped = weights.reshape(CH, 3, 3, 3).transpose(3, 0, 1, 2)
    rows = [
        jnp.pad(shaped, ((0, 0), (0, 0), (x, width - 1 - x), (0, 13))) for x in range(width)
    ]
    return jnp.stack(rows, 1).reshape(3 * width * CH, 128).astype(F32)


def head_taps(weights):
    halves = weights.reshape(3, 1, 2, 1, CH) * jnp.eye(BX, dtype=BF16).reshape(1, BX, 1, BX, 1)
    return jnp.pad(halves.reshape(3 * BX, 2 * BX * CH), ((0, 4), (0, 0)))


def per_device(part_cells, part_offsets, part_counts, w_first, w_mid, w_last, w_head, cotangent):
    n_slab, n_sub = lax.axis_size("slab"), lax.axis_size("sub")
    devices = n_slab * n_sub
    slots = part_cells.shape[2]
    live = jnp.arange(slots, dtype=jnp.int32)[None, :] < part_counts[0][:, None]
    cells = jnp.where(live, part_cells[0], -1).astype(F32).reshape(devices, 2, 128)
    packed = jnp.concatenate([cells, part_offsets[0].reshape(devices, 6, 128)], 1)
    got = lax.all_to_all(packed, ("slab", "sub"), split_axis=0, concat_axis=0, tiled=True)
    ct = cotangent.transpose(2, 0, 1, 3).reshape(BY, 3 * BX, NZ)
    ct = jnp.pad(ct, ((0, 0), (0, 4), (0, 0)))
    head = head_taps(w_head)
    vmem = pl.BlockSpec(memory_space=pltpu.VMEM)
    field = pltpu.VMEM((BY + 2, COLS, NZ), BF16)
    kept = pltpu.VMEM((BY, BX * CH, NZ), F32)
    force, pay = pl.pallas_call(
        body,
        out_shape=(
            jax.ShapeDtypeStruct((BY, 16, NZ), BF16),
            jax.ShapeDtypeStruct((48, 384), F32),
        ),
        in_specs=[vmem] * 9,
        out_specs=(vmem, vmem),
        scratch_shapes=[
            pltpu.VMEM((2, NZ, 256 * GROUP), BF16),
            pltpu.VMEM((2, 192, 256 * GROUP), BF16),
            pltpu.VMEM((48, NZ), F32),
            pltpu.VMEM((5, 48, NZ), F32),
            pltpu.VMEM((128, NZ), F32),
            pltpu.VMEM((128, NZ), BF16),
            field, field, field, field, kept, kept,
            pltpu.VMEM((192, 384), F32),
            pltpu.SemaphoreType.DMA((24,)),
            pltpu.SemaphoreType.DMA((24,)),
            pltpu.SemaphoreType.DMA((5,)),
            pltpu.SemaphoreType.DMA((5,)),
        ],
        compiler_params=pltpu.CompilerParams(
            collective_id=0, has_side_effects=True, vmem_limit_bytes=48 << 20
        ),
        name="level",
    )(
        got, ct, first_taps(w_first), wide_taps(w_mid), wide_taps(w_last),
        wide_taps(flipped(w_mid)), wide_taps(flipped(w_last)), head, head.T,
    )
    loss_scale = 1.0 / math.sqrt(BX * n_slab * BY * n_sub * NZ)
    pay = loss_scale * lax.psum(pay, ("slab", "sub"))
    both = pay[:, :288].reshape(3, CH, 3, 2, 3, CH).transpose(3, 1, 4, 2, 0, 5)
    both = both.reshape(2, CH, 27 * CH)
    first = pay[:, 288:336].reshape(3, CH, 3, 16)[..., :3].transpose(1, 2, 3, 0)
    top = pay[:12, 336:368].reshape(3, BX, 2 * CH).sum(1)
    force = force[:, : 3 * BX].reshape(BY, 3, BX, NZ).transpose(1, 2, 0, 3)
    return force, first.reshape(CH, 27), both[0], both[1], top


def solution(mesh):
    in_specs = (
        P(("slab", "sub"), None, None),
        P(("slab", "sub"), None, None, None),
        P(("slab", "sub"), None),
        P(), P(), P(), P(),
        P(None, "slab", "sub", None),
    )
    out_specs = (P(None, "slab", "sub", None), P(), P(), P(), P())
    return jax.shard_map(
        per_device, mesh=mesh, in_specs=in_specs, out_specs=out_specs, check_vma=False
    )
```

time: 1680 us -> 246 us (0.15)
  other arithmetic: 1410 us -> 10.8 us
  waiting for transfers between devices: 42.6 us -> 137 us
  blocking collectives: 62.7 us -> 0 us
  matrix products: 48.5 us -> 0 us
  Pallas kernels: 0 us -> 48 us
  starting transfers between devices: 55.7 us -> 11.5 us
  local copies, waits for them, and re-layouts: 42.4 us -> 23.7 us
    scatter-add x9 -> x0, other arithmetic: 1390 us -> none  [the longest x8 1390 us: per_device(): padded = padded.at[index.reshape(-1)].add(share.reshape(-1))]
    psum x0 -> x1, waiting for transfers between devices: none -> 137 us  [per_device(): pay = loss_scale * lax.psum(pay, ('slab', 'sub'))]
    psum x1 -> x0, blocking collectives: 62.7 us -> none  [per_device(): lax.psum((grad_first, grad_mid, grad_last, grad_head), ('slab', 'sub'))]
    dot_general x291 -> x0, matrix products: 48.5 us -> none  [the longest x180 29.5 us: conv_planes(): jnp.dot(blocks[:, shift_x, shift_y], piece, preferred_element_type=jnp.fl...]
    pallas_call x0 -> x1, Pallas kernels: none -> 48 us  [per_device(): pl.pallas_call(body, out_shape=(jax.ShapeDtypeStruct((BY, 16, NZ), BF16),...]
    ppermute x22 -> x0, starting transfers between devices: 35.6 us -> none  [the longest x10 26.5 us: padded_2(): after = lax.ppermute(initial, axis, down)]
    ppermute x22 -> x0, waiting for transfers between devices: 21.5 us -> none  [the longest x10 10.6 us: padded_2(): before = lax.ppermute(last, axis, up)]
    all_to_all x3 -> x1, waiting for transfers between devices: 21 us -> 0.01 us  [per_device(): lax.all_to_all(packed, ('slab', 'sub'), split_axis=0, concat_axis=0, tile...]
  transfers between devices with their start and end apart: 25 -> 2, of which waited for: 17 -> 1; matrix products, arithmetic and copies ran while one was open for 3% -> 10% of each run, Pallas kernels for 0% -> 0%
where the time goes in v1:
time: 246 us
  waiting for transfers between devices  137 us (56%)
  Pallas kernels  48 us (20%)
  local copies, waits for them, and re-layouts  23.7 us (10%)
  between operations  14.4 us (6%)
  starting transfers between devices  11.5 us (5%)
  other arithmetic  10.8 us (4%)
    psum x1, waiting for transfers between devices, per_device(): pay = loss_scale * lax.psum(pay, ('slab', 'sub'))  137 us
    pallas_call x1, Pallas kernels, per_device(): pl.pallas_call(body, out_shape=(jax.ShapeDtypeStruct((BY, 16, NZ), BF16),...  48 us
    all_to_all x1, starting transfers between devices, per_device(): lax.all_to_all(packed, ('slab', 'sub'), split_axis=0, concat_axis=0, tile...  11.5 us
    another operation x4, other arithmetic, wide_taps(): return jnp.stack(rows, 1).reshape(3 * BX * CH, 3 * COLS)  8.1 us
    unnamed x29, local copies, waits for them, and re-layouts  7.18 us
    another operation x8, local copies, waits for them, and re-layouts, wide_taps(): return jnp.stack(rows, 1).reshape(3 * BX * CH, 3 * COLS)  6.25 us
  transfers between devices with their start and end apart: 2, of which 1 were waited for; matrix products, arithmetic and copies ran while one was open for 10% of the time, Pallas kernels for 0%

profile of v1, /device:TPU:1, one launch (start us, length us, event | category | flops | bytes accessed | tf_op | source)
XLA Modules:
  0.0 245.9 jit_solution(13560012851158772295)
XLA Ops:
  7.2 1.2 copy.63
  8.4 0.2 copy.64
  8.7 0.1 squeeze.9
  8.7 0.2 fusion
  9.0 0.9 pad_maximum_fusion.4
  9.9 11.5 %all-to-all-start = ((f32[128,8,128]{2,1,0:T(8,128)}), f32[128,8,128]{2,1,0:T(8,128)S(1)}, u32[]{:S(2)}, u32[]{:S(2)}) async-start(f32[128,8,128]{2,1,0:T(8,128)} %pad_maximum_fusion.4), calls=%async_computation | async-start | bytes 1048576 | tf_op jit(solution)/shard_map/all_to_all | solution.py:320
  21.4 0.1 copy.66
  21.6 0.2 copy.67
  21.7 0.7 bitcast_dynamic-update-slice_fusion.4
  22.4 0.7 bitcast_dynamic-update-slice_fusion.3
  23.1 0.7 bitcast_dynamic-update-slice_fusion.2
  23.7 0.7 bitcast_dynamic-update-slice_fusion.1
  24.4 0.7 bitcast_dynamic-update-slice_fusion
  25.1 0.1 reshape.93
  25.2 0.5 rev.6
  25.7 0.3 pad_bitcast_fusion.7
  26.1 0.1 reshape.95
  26.3 0.5 rev.7
  26.7 0.3 pad_bitcast_fusion.3
  27.1 0.3 pad_bitcast_fusion.15
  27.5 0.3 pad_bitcast_fusion.11
  27.8 1.2 pad_maximum_fusion.2
  29.0 2.3 pad_maximum_fusion.3
  31.3 2.3 pad_maximum_fusion
  33.6 2.3 pad_maximum_fusion.1
  35.9 0.7 bitcast_dynamic-update-slice_fusion.5
  36.6 1.5 reshape.104.w_one
  38.1 1.1 copy.75
  39.2 0.5 reshape.97
  39.8 0.1 copy.80.w_mid_t
  39.9 0.6 copy-done
  40.5 1.1 copy.76
  41.7 0.5 reshape.98
  42.2 0.1 copy.81.w_last_t
  42.3 0.6 copy-done.1
  42.9 1.4 copy.73
  44.3 0.5 reshape.94
  44.9 0.1 copy.78.w_mid
  45.0 0.6 copy-done.2
  45.6 1.2 copy.74
  46.8 0.5 reshape.96
  47.3 0.1 copy.79.w_last
  47.5 0.1 mul.25
  47.6 0.1 broadcast_multiply_fusion.1
  47.7 0.1 mul.29
  47.8 0.1 copy.77
  47.9 0.1 copy.88
  48.0 0.1 copy.65
  48.1 48.0 %level.1 = (bf16[8,16,256]{2,1,0:T(8,128)(2,1)S(1)}, f32[48,384]{1,0:T(8,128)}) custom-call(f32[128,8,128]{2,1,0:T(8,128)S(1)} %all-to-all-done.got, bf16[8,16,256]{2,1,0:T(8,128)(2,1)S(1)} %pad.84.ct, f32[288,128]{1,0:T(8,128)S(1)} %reshape.104.w_one, bf16[192,288]{1,0:T(8,128)(2,1)S(1)} %copy.78.w_mid, bf16[192,288]{1,0:T(8,128)(2,1)S(1)} %copy.79.w_last, ...), custom_call_target="tpu_custom_call" | custom-call | tf_op jit(solution)/shard_map/level/pallas_call | solution.py:327
  96.1 0.6 copy.83
  96.8 137.4 %all-reduce.26.cloned.1.call-done = f32[48,384]{1,0:T(8,128)} async-done(((f32[48,384]{1,0:T(8,128)}), f32[48,384]{1,0:T(8,128)}) %all-reduce.26.cloned.1.call-update) | async-done | bytes 73744 | tf_op jit(solution)/shard_map/psum | solution.py:358
  234.2 0.9 broadcast_multiply_fusion
  235.1 0.1 slice.30
  235.1 0.1 slice.35
  235.2 0.3 reshape.102
  235.5 0.1 fusion.2
  235.6 0.2 copy.85
  235.8 0.8 squeeze.10
  236.6 0.2 copy.86
  236.7 0.8 squeeze.11
  237.5 0.1 reshape.100
  237.6 0.1 copy.84
  237.8 0.7 copy.87
  238.5 0.6 reduce_sum.9
  (29 shorter events, 0.2 us)
Async XLA Ops:
  7.2 1.5 copy-start.3
  7.2 1.6 copy-start.9
  9.0 12.5 %copy-start.7 = (bf16[16,27]{1,0:T(8,128)(2,1)S(1)}, bf16[16,27]{1,0:T(8,128)(2,1)}, u32[]{:S(2)}) copy-start(bf16[16,27]{1,0:T(8,128)(2,1)} %param.11) | copy-start | bytes 2596
  9.9 15.2 %copy-start.5 = (bf16[16,432]{1,0:T(8,128)(2,1)S(1)}, bf16[16,432]{1,0:T(8,128)(2,1)}, u32[]{:S(2)}) copy-start(bf16[16,432]{1,0:T(8,128)(2,1)} %param.12) | copy-start | bytes 41476
  9.9 38.2 %all-to-all-start = ((f32[128,8,128]{2,1,0:T(8,128)}), f32[128,8,128]{2,1,0:T(8,128)S(1)}, u32[]{:S(2)}, u32[]{:S(2)}) async-start(f32[128,8,128]{2,1,0:T(8,128)} %pad_maximum_fusion.4), calls=%async_computation | async-start | bytes 1048576 | tf_op jit(solution)/shard_map/all_to_all | solution.py:320
  21.4 212.8 %all-reduce.26.cloned.1.call-start = ((), (), s32[]{:S(2)}) async-start(), calls=%async_computation.1 | async-start | bytes 147456 | tf_op jit(solution)/shard_map/psum | solution.py:358
  22.4 3.7 %copy-start.6 = (bf16[16,432]{1,0:T(8,128)(2,1)S(1)}, bf16[16,432]{1,0:T(8,128)(2,1)}, u32[]{:S(2)}) copy-start(bf16[16,432]{1,0:T(8,128)(2,1)} %param.13) | copy-start | bytes 41476
  39.2 1.3 copy-start
  41.6 1.3 copy-start.1
  44.3 1.3 copy-start.2
  45.6 1.9 copy-start.8
  46.8 1.2 copy-start.4
Sparse Core Ops, SparseCore 0:
  96.3 137.8 all-reduce.25

commit v2 on v1

--- a/solution.py
+++ b/solution.py
@@ -89,18 +89,33 @@
 
 
 def body(
-    got, ct, w_one, w_mid, w_last, w_mid_t, w_last_t, w_head, w_head_t,
-    force, pay,
+    got, ct, w_first, w_mid_in, w_last_in, w_head_in,
+    force, grad_first, grad_mid, grad_last, grad_head,
     hot_s, wt_s, dep, dep_in, dens_f, dens, one, two, g_three, g_two, pre_one, pre_two, acc,
-    send, recv, send_d, recv_d,
+    base, w_one, w_mid, w_last, w_mid_t, w_last_t, head_f, head_b, ct_s, pay, half_in, ring, whole,
+    send, recv, send_d, recv_d, send_s, recv_s,
 ):
     n_slab, n_sub = lax.axis_size("slab"), lax.axis_size("sub")
     slab, sub = lax.axis_index("slab"), lax.axis_index("sub")
     up, down, other = (slab + 1) % n_slab, (slab + n_slab - 1) % n_slab, (sub + 1) % n_sub
     neighbours = ((up, sub), (down, sub), (slab, other), (up, other), (down, other))
+    axes = []
+    for stride in (1, 4, 16):
+        size = min(4, max(1, n_slab // stride))
+        at = slab // stride % size
+        axes.append((at, [slab + ((at + i) % size - at) * stride for i in range(1, size)]))
+    partners = [(peer, sub) for _, peers in axes for peer in peers]
     barrier = pltpu.get_barrier_semaphore()
-    for device in neighbours:
+    for device in (*neighbours, *partners):
         pl.semaphore_signal(barrier, inc=1, device_id=device, device_id_type=MESH)
+
+    make_tables(w_first, w_mid_in, w_last_in, w_head_in, base, w_one, w_mid, w_last, w_mid_t,
+                w_last_t, head_f, head_b)
+    ct_s[...] = jnp.zeros_like(ct_s)
+    for k in range(3):
+        for x in range(BX):
+            at = (k * BX + x) * BY
+            ct_s[at : at + BY] = ct[k, x]
 
     dep2 = jnp.zeros((96, NZ), F32)
     sources = got.shape[0]
@@ -121,7 +136,7 @@
     dep2 = lax.fori_loop(0, sources // (2 * GROUP), gather, dep2)
     dep[...] = dep2[:48] + lane_roll(dep2[48:], 1)
 
-    pl.semaphore_wait(barrier, len(neighbours))
+    pl.semaphore_wait(barrier, len(neighbours) + len(partners))
 
     def remote(src, dst, at, device, sends, recvs):
         return pltpu.make_async_remote_copy(
@@ -208,19 +223,25 @@
     for copy in rims(two, 0):
         copy.wait()
 
-    heads = []
+    row_y = lax.broadcasted_iota(jnp.int32, (128, 128), 0) % BY
+    lane_y = lax.broadcasted_iota(jnp.int32, (128, 128), 1) % BY
+    out = jnp.zeros((96, NZ), F32)
+    head = jnp.zeros((128, 128), F32)
     for y in range(BY):
         pre = conv(w_last, two, y)
         s = sigmoid(pre)
         features = jnp.concatenate([(pre * s).astype(BF16), one[y + 1, CORE]], 0)
-        force[y] = dot(w_head[...], features).astype(BF16)
-        heads.append((ct[y], features))
-        back = dot(w_head_t[: BX * CH], ct[y])
+        taps = jnp.where(row_y == y, head_f[...], 0.0)[:96].astype(BF16)
+        out = out + dot(taps, features)
+        head = head + jnp.where(row_y == y, dot_nt(ct_s[...], features), 0.0)
+        taps = jnp.where(lane_y == y, head_b[...], 0.0)[: BX * CH].astype(BF16)
+        back = dot(taps, ct_s[...])
         g_three[y + 1, CORE] = (back * (s * (1.0 + pre * (1.0 - s)))).astype(BF16)
     started = rims(g_three, 8)
-    head = dot_nt(*heads[0])
-    for pair in heads[1:]:
-        head = head + dot_nt(*pair)
+    for k in range(3):
+        for x in range(BX):
+            at = (k * BX + x) * BY
+            force[k, x] = out[at : at + BY].astype(BF16)
 
     def weight_grad(grads, field, shift):
         acc[:, 3 * COLS :] = jnp.zeros((192, 96), F32)
@@ -256,7 +277,8 @@
 
     first = jnp.zeros((192, 128), F32)
     for y in range(BY):
-        back = conv(w_mid_t, g_two, y) + dot(w_head_t[BX * CH :], ct[y])
+        taps = jnp.where(lane_y == y, head_b[...], 0.0)[BX * CH :].astype(BF16)
+        back = conv(w_mid_t, g_two, y) + dot(taps, ct_s[...])
         grad = (back * slope(pre_one[y])).astype(BF16).astype(F32)
         first = first + lane_roll(dot_nt(spread_z(grad), dens[...]), -y)
     rows = []
@@ -270,44 +292,112 @@
     lane = lax.broadcasted_iota(jnp.int32, joint.shape, 1)
     joint = jnp.where((lane % 16 < 3) & (lane < 48), joint, 0.0)
     extra = lane_roll(joint, 32)
-    lane = lax.broadcasted_iota(jnp.int32, (16, 128), 1)
-    row = lax.broadcasted_iota(jnp.int32, (16, 128), 0)
-    total = jnp.zeros((16, 128), F32)
-    for x in range(BX):
-        mine = (row % BX == x) & (lane % 64 < CH)
-        total = total + jnp.where(mine, lane_roll(head, -CH * x), 0.0)
-    total = jnp.where(lane < CH, total, 0.0) + jnp.where(
-        (lane >= CH) & (lane < 2 * CH), lane_roll(total, -48), 0.0
+    row = lax.broadcasted_iota(jnp.int32, (128, 128), 0)
+    lane = lax.broadcasted_iota(jnp.int32, (128, 128), 1)
+    head = jnp.where(lane % 64 // CH == row // BY % BX, head, 0.0)
+    kept = jnp.concatenate(
+        [jnp.sum(head[k * 32 : k * 32 + 32], 0, keepdims=True) for k in range(3)]
+        + [jnp.zeros((5, 128), F32)],
+        0,
     )
-    total = lane_roll(total, 80)
+    kept = kept + lane_roll(kept, -2 * CH)
+    kept = kept + lane_roll(kept, -CH)
+    lane = lax.broadcasted_iota(jnp.int32, (8, 128), 1)
+    top = jnp.where(lane < CH, kept, 0.0) + jnp.where(
+        (lane >= CH) & (lane < 2 * CH), lane_roll(kept, -48), 0.0
+    )
+    top = lane_roll(top, 80)
     pay[...] = sums
     pay[:, 256:384] += extra
-    pay[:16, 256:384] += total
-
-
-def wide_taps(weights):
-    shaped = weights.reshape(CH, 3, 3, 3, CH).transpose(3, 0, 2, 1, 4)
-    rows = [jnp.pad(shaped, ((0, 0), (0, 0), (0, 0), (x, BX - 1 - x), (0, 0))) for x in range(BX)]
-    return jnp.stack(rows, 1).reshape(3 * BX * CH, 3 * COLS)
-
-
-def flipped(weights):
-    shaped = weights.reshape(CH, 3, 3, 3, CH)[:, ::-1, ::-1, ::-1]
-    return shaped.transpose(4, 1, 2, 3, 0).reshape(CH, 27 * CH)
-
-
-def first_taps(weights):
-    width = BX + 2
-    shaped = weights.reshape(CH, 3, 3, 3).transpose(3, 0, 1, 2)
-    rows = [
-        jnp.pad(shaped, ((0, 0), (0, 0), (x, width - 1 - x), (0, 13))) for x in range(width)
-    ]
-    return jnp.stack(rows, 1).reshape(3 * width * CH, 128).astype(F32)
-
-
-def head_taps(weights):
-    halves = weights.reshape(3, 1, 2, 1, CH) * jnp.eye(BX, dtype=BF16).reshape(1, BX, 1, BX, 1)
-    return jnp.pad(halves.reshape(3 * BX, 2 * BX * CH), ((0, 4), (0, 0)))
+    pay[:8, 256:384] += top
+
+    theirs = pl.ds(pl.multiple_of(other * 24, 8), 24)
+    mine = pl.ds(pl.multiple_of(sub * 24, 8), 24)
+    copy = remote(pay.at[theirs], half_in, 0, (slab, other), send_s, recv_s)
+    copy.start()
+    copy.wait()
+    total = pay[mine] + half_in[...]
+    at_sem = 1
+    for turn in range(3):
+        copies = []
+        for part in range(3):
+            at, peers = axes[(part + turn) % 3]
+            rows = pl.ds(part * 8, 8)
+            ring[turn, at, rows] = total[part * 8 : part * 8 + 8]
+            for peer in peers:
+                slot = ring.at[turn, at, rows]
+                copies.append(remote(slot, slot, at_sem, (peer, sub), send_s, recv_s))
+                copies[-1].start()
+                at_sem += 1
+        for copy in copies:
+            copy.wait()
+        parts = []
+        for part in range(3):
+            size = len(axes[(part + turn) % 3][1]) + 1
+            rows = slice(part * 8, part * 8 + 8)
+            value = ring[turn, 0, rows]
+            for slot in range(1, size):
+                value = value + ring[turn, slot, rows]
+            parts.append(value)
+        total = jnp.concatenate(parts, 0)
+    whole[mine] = total * (1.0 / math.sqrt(BX * n_slab * BY * n_sub * NZ))
+    copy = remote(whole.at[mine], whole.at[mine], at_sem, (slab, other), send_s, recv_s)
+    copy.start()
+    copy.wait()
+    for dx, dy, dz in OFFSETS:
+        rows, tap = slice(dz * CH, dz * CH + CH), dx * 9 + dy * 3 + dz
+        at, to = dy * 96 + dx * CH, slice(tap * CH, tap * CH + CH)
+        grad_mid[:, to] = whole[rows, at : at + CH]
+        grad_last[:, to] = whole[rows, at + 48 : at + 48 + CH]
+        at = 288 + dx * CH + dy
+        grad_first[:, tap : tap + 1] = whole[rows, at : at + 1]
+    grad_head[...] = whole[:3, 336:368]
+
+
+OFFSETS = [(dx, dy, dz) for dx in range(3) for dy in range(3) for dz in range(3)]
+
+
+def make_tables(w_first, w_mid, w_last, w_head, base, one, mid, last, mid_t, last_t, head_f, head_b):
+    def spread(out):
+        for dz in range(3):
+            for x in range(BX):
+                at = (dz * BX + x) * CH
+                moved = lane_roll(base[dz * CH : dz * CH + CH], x * CH)
+                out[at : at + CH] = moved[:, : 3 * COLS].astype(BF16)
+
+    base[...] = jnp.zeros_like(base)
+    for source, out, out_t in ((w_mid, mid, mid_t), (w_last, last, last_t)):
+        weights = source[...].astype(F32)
+        for dx, dy, dz in OFFSETS:
+            tap, at = dx * 9 + dy * 3 + dz, dy * 96 + dx * CH
+            base[dz * CH : dz * CH + CH, at : at + CH] = weights[:, tap * CH : tap * CH + CH]
+        spread(out)
+        padded = jnp.concatenate([weights, jnp.zeros((CH, 80), F32)], 1)
+        turned = jnp.concatenate([padded, jnp.zeros((112, 512), F32)], 0).T
+        for dx, dy, dz in OFFSETS:
+            tap, at = dx * 9 + dy * 3 + dz, (2 - dy) * 96 + (2 - dx) * CH
+            to = (2 - dz) * CH
+            base[to : to + CH, at : at + CH] = turned[tap * CH : tap * CH + CH, :CH]
+        spread(out_t)
+    base[...] = jnp.zeros_like(base)
+    weights = w_first[...].astype(F32)
+    for dx, dy, dz in OFFSETS:
+        tap, at = dx * 9 + dy * 3 + dz, dx * 16 + dy
+        base[dz * CH : dz * CH + CH, at : at + 1] = weights[:, tap : tap + 1]
+    for dz in range(3):
+        for x in range(BX + 2):
+            at = (dz * (BX + 2) + x) * CH
+            one[at : at + CH] = lane_roll(base[dz * CH : dz * CH + CH, :128], x * 16)
+    head_f[...] = jnp.zeros_like(head_f)
+    weights = w_head[...].astype(F32)
+    for k in range(3):
+        for x in range(BX):
+            at = (k * BX + x) * BY
+            for half in range(2):
+                row = weights[k : k + 1, half * CH : half * CH + CH]
+                to = half * 64 + x * CH
+                head_f[at : at + BY, to : to + CH] = jnp.broadcast_to(row, (BY, CH))
+    head_b[...] = head_f[...].T
 
 
 def per_device(part_cells, part_offsets, part_counts, w_first, w_mid, w_last, w_head, cotangent):
@@ -318,20 +408,21 @@
     cells = jnp.where(live, part_cells[0], -1).astype(F32).reshape(devices, 2, 128)
     packed = jnp.concatenate([cells, part_offsets[0].reshape(devices, 6, 128)], 1)
     got = lax.all_to_all(packed, ("slab", "sub"), split_axis=0, concat_axis=0, tiled=True)
-    ct = cotangent.transpose(2, 0, 1, 3).reshape(BY, 3 * BX, NZ)
-    ct = jnp.pad(ct, ((0, 0), (0, 4), (0, 0)))
-    head = head_taps(w_head)
     vmem = pl.BlockSpec(memory_space=pltpu.VMEM)
     field = pltpu.VMEM((BY + 2, COLS, NZ), BF16)
     kept = pltpu.VMEM((BY, BX * CH, NZ), F32)
-    force, pay = pl.pallas_call(
+    table = pltpu.VMEM((192, 3 * COLS), BF16)
+    return pl.pallas_call(
         body,
         out_shape=(
-            jax.ShapeDtypeStruct((BY, 16, NZ), BF16),
-            jax.ShapeDtypeStruct((48, 384), F32),
+            jax.ShapeDtypeStruct(cotangent.shape, BF16),
+            jax.ShapeDtypeStruct(w_first.shape, F32),
+            jax.ShapeDtypeStruct(w_mid.shape, F32),
+            jax.ShapeDtypeStruct(w_last.shape, F32),
+            jax.ShapeDtypeStruct(w_head.shape, F32),
         ),
-        in_specs=[vmem] * 9,
-        out_specs=(vmem, vmem),
+        in_specs=[vmem] * 6,
+        out_specs=[vmem] * 5,
         scratch_shapes=[
             pltpu.VMEM((2, NZ, 256 * GROUP), BF16),
             pltpu.VMEM((2, 192, 256 * GROUP), BF16),
@@ -341,27 +432,28 @@
             pltpu.VMEM((128, NZ), BF16),
             field, field, field, field, kept, kept,
             pltpu.VMEM((192, 384), F32),
+            pltpu.VMEM((48, 384), F32),
+            pltpu.VMEM((288, 128), F32),
+            table, table, table, table,
+            pltpu.VMEM((128, 128), F32),
+            pltpu.VMEM((128, 128), F32),
+            pltpu.VMEM((128, NZ), BF16),
+            pltpu.VMEM((48, 384), F32),
+            pltpu.VMEM((24, 384), F32),
+            pltpu.VMEM((3, 4, 24, 384), F32),
+            pltpu.VMEM((48, 384), F32),
             pltpu.SemaphoreType.DMA((24,)),
             pltpu.SemaphoreType.DMA((24,)),
             pltpu.SemaphoreType.DMA((5,)),
             pltpu.SemaphoreType.DMA((5,)),
+            pltpu.SemaphoreType.DMA((29,)),
+            pltpu.SemaphoreType.DMA((29,)),
         ],
         compiler_params=pltpu.CompilerParams(
             collective_id=0, has_side_effects=True, vmem_limit_bytes=48 << 20
         ),
         name="level",
-    )(
-        got, ct, first_taps(w_first), wide_taps(w_mid), wide_taps(w_last),
-        wide_taps(flipped(w_mid)), wide_taps(flipped(w_last)), head, head.T,
-    )
-    loss_scale = 1.0 / math.sqrt(BX * n_slab * BY * n_sub * NZ)
-    pay = loss_scale * lax.psum(pay, ("slab", "sub"))
-    both = pay[:, :288].reshape(3, CH, 3, 2, 3, CH).transpose(3, 1, 4, 2, 0, 5)
-    both = both.reshape(2, CH, 27 * CH)
-    first = pay[:, 288:336].reshape(3, CH, 3, 16)[..., :3].transpose(1, 2, 3, 0)
-    top = pay[:12, 336:368].reshape(3, BX, 2 * CH).sum(1)
-    force = force[:, : 3 * BX].reshape(BY, 3, BX, NZ).transpose(1, 2, 0, 3)
-    return force, first.reshape(CH, 27), both[0], both[1], top
+    )(got, cotangent, w_first, w_mid, w_last, w_head)
 
 
 def solution(mesh):

time: 246 us -> 92.7 us (0.38)
  waiting for transfers between devices: 137 us -> 0 us
  blocking collectives: 0 us -> 25 us
  local copies, waits for them, and re-layouts: 23.7 us -> 6.07 us
  between operations: 14.4 us -> 0.74 us
  Pallas kernels: 48 us -> 60.3 us
  starting transfers between devices: 11.5 us -> 0 us
  other arithmetic: 10.8 us -> 0.32 us
    psum x1 -> x0, waiting for transfers between devices: 137 us -> none  [per_device(): pay = loss_scale * lax.psum(pay, ('slab', 'sub'))]
    all_to_all x0 -> x1, blocking collectives: none -> 25 us  [per_device(): lax.all_to_all(packed, ('slab', 'sub'), split_axis=0, concat_axis=0, tile...]
    pallas_call x1, Pallas kernels: 48 us -> 60.3 us  [per_device(): pl.pallas_call(body, out_shape=(jax.ShapeDtypeStruct(cotangent.shape, BF1...]
    all_to_all x1 -> x0, starting transfers between devices: 11.5 us -> none  [per_device(): lax.all_to_all(packed, ('slab', 'sub'), split_axis=0, concat_axis=0, tile...]
    another operation x4 -> x0, other arithmetic: 8.1 us -> none  [wide_taps(): return jnp.stack(rows, 1).reshape(3 * BX * CH, 3 * COLS)]
    another operation x9 -> x0, local copies, waits for them, and re-layouts: 6.93 us -> none  [the longest x8 6.25 us: wide_taps(): return jnp.stack(rows, 1).reshape(3 * BX * CH, 3 * COLS)]
    reshape x17 -> x0, local copies, waits for them, and re-layouts: 3.6 us -> none  [the longest x8 2.69 us: wide_taps(): return jnp.stack(rows, 1).reshape(3 * BX * CH, 3 * COLS)]
    unnamed x29 -> x18, local copies, waits for them, and re-layouts: 7.18 us -> 4.86 us
  transfers between devices with their start and end apart: 2 -> 0, of which waited for: 1 -> 0; matrix products, arithmetic and copies ran while one was open for 10% -> 0% of each run, Pallas kernels for 0% -> 0%
where the time goes in v2:
time: 92.7 us; the launch traced here: 92.5 us
  Pallas kernels  60.3 us (65%)
  blocking collectives  25 us (27%)
  local copies, waits for them, and re-layouts  6.07 us (7%)
    pallas_call x1, Pallas kernels, per_device(): pl.pallas_call(body, out_shape=(jax.ShapeDtypeStruct(cotangent.shape, BF1...  60.3 us
    all_to_all x1, blocking collectives, per_device(): lax.all_to_all(packed, ('slab', 'sub'), split_axis=0, concat_axis=0, tile...  25 us
    unnamed x18, local copies, waits for them, and re-layouts  4.86 us

profile of v2, /device:TPU:1, one launch (start us, length us, event | category | flops | bytes accessed | tf_op | source)
XLA Modules:
  0.0 92.5 jit_solution(6510795245350076411)
XLA Ops:
  0.6 1.0 %squeeze.3 = s32[128,2,128]{2,1,0:T(2,128)S(1)} reshape(s32[1,128,256]{2,1,0:T(8,128)} %param.8) | data formatting | bytes 262144 | tf_op jit(solution)/shard_map/squeeze | solution.py:408
  1.6 1.2 %copy.14 = f32[1,128,3,256]{1,3,2,0:T(8,128)S(1)} copy(f32[1,128,3,256]{3,1,2,0:T(8,128)} %param.9) | data formatting | bytes 786432 | tf_op args[1]
  2.8 0.2 copy.15
  3.0 0.0 copy-start.5
  3.0 0.6 copy-done.5
  3.7 0.2 fusion
  3.9 0.1 pad_maximum_fusion
  4.0 0.0 copy-start
  4.0 0.0 copy-start.1
  4.0 0.0 copy-start.2
  4.0 0.0 copy-start.3
  4.1 0.0 copy-start.4
  4.1 25.0 %all_to_all.5.got = f32[128,8,128]{2,1,0:T(8,128)S(1)} all-to-all(f32[128,8,128]{2,1,0:T(8,128)S(1)} %pad_maximum_fusion), channel_id=1, replica_groups=mesh['slab'=64,'sub'=2] {'slab','sub'}, dimensions={0} | all-to-all | bytes 1048576 | tf_op jit(solution)/shard_map/all_to_all | solution.py:410
  29.1 0.0 copy-done
  29.1 0.0 copy-done.1
  29.1 0.0 copy-done.2
  29.1 0.0 copy-done.3
  29.1 0.0 copy-done.4
  29.1 60.3 %level.1 = (bf16[3,4,8,256]{3,2,1,0:T(8,128)(2,1)S(1)}, f32[16,27]{1,0:T(8,128)S(1)}, f32[16,432]{1,0:T(8,128)S(1)}, f32[16,432]{1,0:T(8,128)S(1)}, f32[3,32]{1,0:T(4,128)S(1)}) custom-call(f32[128,8,128]{2,1,0:T(8,128)S(1)} %all_to_all.5.got, bf16[3,4,8,256]{3,2,1,0:T(8,128)(2,1)S(1)} %copy-done, bf16[16,27]{1,0:T(8,128)(2,1)S(1)} %copy-done.3, ...), custom_call_target="tpu_custom_call" | custom-call | tf_op jit(solution)/shard_map/level/pallas_call | solution.py:415
  89.4 0.6 copy.21
  90.1 0.6 copy.22
  90.7 0.6 copy.23
  91.3 0.6 copy.24
  91.9 0.6 copy.25
  (1 shorter events, 0.0 us)
Async XLA Ops:
  3.0 0.7 copy-start.5
  4.0 25.1 %copy-start = (bf16[3,4,8,256]{3,2,1,0:T(8,128)(2,1)S(1)}, bf16[3,4,8,256]{3,2,1,0:T(8,128)(2,1)}, u32[]{:S(2)}) copy-start(bf16[3,4,8,256]{3,2,1,0:T(8,128)(2,1)} %ct.1) | copy-start | bytes 147460
  4.0 25.1 %copy-start.1 = (bf16[16,432]{1,0:T(8,128)(2,1)S(1)}, bf16[16,432]{1,0:T(8,128)(2,1)}, u32[]{:S(2)}) copy-start(bf16[16,432]{1,0:T(8,128)(2,1)} %w_mid_in.1) | copy-start | bytes 41476
  4.0 25.1 %copy-start.2 = (bf16[16,432]{1,0:T(8,128)(2,1)S(1)}, bf16[16,432]{1,0:T(8,128)(2,1)}, u32[]{:S(2)}) copy-start(bf16[16,432]{1,0:T(8,128)(2,1)} %w_last_in.1) | copy-start | bytes 41476
  4.0 25.1 %copy-start.3 = (bf16[16,27]{1,0:T(8,128)(2,1)S(1)}, bf16[16,27]{1,0:T(8,128)(2,1)}, u32[]{:S(2)}) copy-start(bf16[16,27]{1,0:T(8,128)(2,1)} %w_first.1) | copy-start | bytes 2596
  4.1 25.1 %copy-start.4 = (bf16[3,32]{1,0:T(4,128)(2,1)S(1)}, bf16[3,32]{1,0:T(4,128)(2,1)}, u32[]{:S(2)}) copy-start(bf16[3,32]{1,0:T(4,128)(2,1)} %w_head_in.1) | copy-start | bytes 580

commit v3 on v2

--- a/solution.py
+++ b/solution.py
@@ -16,6 +16,7 @@
 COLS = (BX + 2) * CH
 CORE = slice(CH, CH + BX * CH)
 GROUP = 4
+SPREAD = 1
 X_ROW = (0, 8, 24, 32, 40)
 
 
@@ -59,15 +60,16 @@
     def spread(value, row, rows=8):
         return jnp.broadcast_to(value[row : row + 1], (rows, 128))
 
-    z_at = spread(where_z, half, NZ).astype(BF16)
+    at = 4 * half
+    z_at = spread(where_z, at + 3, NZ).astype(BF16)
     lanes_z = lax.broadcasted_iota(jnp.int32, (NZ, 128), 0).astype(F32).astype(BF16)
     hot = jnp.where(lanes_z == z_at, jnp.ones((), BF16), jnp.zeros((), BF16))
-    at = spread(plane, half)
-    at_x = lax.shift_right_arithmetic(at, 3)
-    at_y = at & 7
-    f = spread(tile, 2 + half)
-    g = spread(tile, 4 + half)
-    h = spread(tile, 6 + half)
+    plane = spread(plane, at + 3)
+    at_x = lax.shift_right_arithmetic(plane, 3)
+    at_y = plane & 7
+    f = spread(tile, at)
+    g = spread(tile, at + 1)
+    h = spread(tile, at + 2)
     row = lax.broadcasted_iota(jnp.int32, (8, 128), 0)
     zero = jnp.zeros((8, 128), F32)
     weight_y = jnp.where(row == at_y, 1.0 - g, jnp.where(row == at_y + 1, g, zero))
@@ -89,25 +91,57 @@
 
 
 def body(
-    got, ct, w_first, w_mid_in, w_last_in, w_head_in,
+    cells, offsets, counts, ct, w_first, w_mid_in, w_last_in, w_head_in,
     force, grad_first, grad_mid, grad_last, grad_head,
-    hot_s, wt_s, dep, dep_in, dens_f, dens, one, two, g_three, g_two, pre_one, pre_two, acc,
+    packed, got, hot_s, wt_s, dep, dep_in, dens_f, dens, one, two, g_three, g_two, pre_one, pre_two, acc,
     base, w_one, w_mid, w_last, w_mid_t, w_last_t, head_f, head_b, ct_s, pay, half_in, ring, whole,
-    send, recv, send_d, recv_d, send_s, recv_s,
+    send, recv, send_d, recv_d, send_s, recv_s, send_p, recv_p,
 ):
     n_slab, n_sub = lax.axis_size("slab"), lax.axis_size("sub")
     slab, sub = lax.axis_index("slab"), lax.axis_index("sub")
     up, down, other = (slab + 1) % n_slab, (slab + n_slab - 1) % n_slab, (sub + 1) % n_sub
     neighbours = ((up, sub), (down, sub), (slab, other), (up, other), (down, other))
+    devices = n_slab * n_sub
+    me = slab * n_sub + sub
     axes = []
     for stride in (1, 4, 16):
         size = min(4, max(1, n_slab // stride))
         at = slab // stride % size
         axes.append((at, [slab + ((at + i) % size - at) * stride for i in range(1, size)]))
-    partners = [(peer, sub) for _, peers in axes for peer in peers]
+
+    def partner(turn):
+        to = (me + turn * SPREAD) % devices
+        return (to // n_sub, to % n_sub), to
+
     barrier = pltpu.get_barrier_semaphore()
-    for device in (*neighbours, *partners):
-        pl.semaphore_signal(barrier, inc=1, device_id=device, device_id_type=MESH)
+
+    def greet(turn, carry):
+        pl.semaphore_signal(barrier, inc=1, device_id=partner(turn)[0], device_id_type=MESH)
+        return carry
+
+    lax.fori_loop(1, devices, greet, 0)
+
+    diagonal = lax.broadcasted_iota(jnp.int32, (devices, devices), 0) == lax.broadcasted_iota(
+        jnp.int32, (devices, devices), 1
+    )
+    used = jnp.broadcast_to(counts[...].astype(F32), (devices, devices))
+    used = jnp.sum(jnp.where(diagonal, used, 0.0), 1, keepdims=True)
+    slot = lax.broadcasted_iota(jnp.int32, (devices, 256), 1).astype(F32)
+    live = jnp.where(slot < used, cells[0].astype(F32), -1.0)
+    for first in range(0, devices, 8):
+        for half in range(2):
+            rows = pl.ds(first * 8 + 4 * half + 3, 8, stride=8)
+            packed[rows, :] = live[first : first + 8, half * 128 : half * 128 + 128]
+
+    def pack(step, carry):
+        for k in range(8):
+            to = step * 8 + k
+            for half in range(2):
+                rows = pl.ds(to * 8 + 4 * half, 3)
+                packed[rows, :] = offsets[0, to, :, half * 128 : half * 128 + 128]
+        return carry
+
+    lax.fori_loop(0, devices // 8, pack, 0)
 
     make_tables(w_first, w_mid_in, w_last_in, w_head_in, base, w_one, w_mid, w_last, w_mid_t,
                 w_last_t, head_f, head_b)
@@ -117,13 +151,39 @@
             at = (k * BX + x) * BY
             ct_s[at : at + BY] = ct[k, x]
 
-    dep2 = jnp.zeros((96, NZ), F32)
-    sources = got.shape[0]
+    def remote(src, dst, at, device, sends, recvs):
+        return pltpu.make_async_remote_copy(
+            src_ref=src, dst_ref=dst, send_sem=sends.at[at], recv_sem=recvs.at[at],
+            device_id=device, device_id_type=MESH,
+        )
+
+    pl.semaphore_wait(barrier, devices - 1)
+
+    def tile_rows(at):
+        return pl.ds(pl.multiple_of(at * 8, 8), 8)
+
+    def tile_copy(turn):
+        device, to = partner(turn)
+        return remote(
+            packed.at[tile_rows(to)], got.at[tile_rows(turn)], turn, device, send_p, recv_p
+        )
+
+    def send_tile(turn, carry):
+        tile_copy(turn).start()
+        return carry
+
+    lax.fori_loop(1, devices, send_tile, 0)
+    got[:8] = packed[tile_rows(me)]
+
+    def take(turn, carry):
+        tile_copy(turn).wait_recv()
+        return carry
 
     def gather(step, total):
+        lax.fori_loop(jnp.maximum(step * 2 * GROUP, 1), (step + 1) * 2 * GROUP, take, 0)
         for part in range(2):
             for k in range(GROUP):
-                tile = got[step * 2 * GROUP + part * GROUP + k]
+                tile = got[tile_rows(step * 2 * GROUP + part * GROUP + k)]
                 for half in range(2):
                     hot, weights = source_terms(tile, half)
                     at = k * 256 + half * 128
@@ -133,16 +193,14 @@
             total = total + result[:96] + result[96:]
         return total
 
-    dep2 = lax.fori_loop(0, sources // (2 * GROUP), gather, dep2)
+    dep2 = lax.fori_loop(0, devices // (2 * GROUP), gather, jnp.zeros((96, NZ), F32))
     dep[...] = dep2[:48] + lane_roll(dep2[48:], 1)
 
-    pl.semaphore_wait(barrier, len(neighbours) + len(partners))
-
-    def remote(src, dst, at, device, sends, recvs):
-        return pltpu.make_async_remote_copy(
-            src_ref=src, dst_ref=dst, send_sem=sends.at[at], recv_sem=recvs.at[at],
-            device_id=device, device_id_type=MESH,
-        )
+    def sent(turn, carry):
+        tile_copy(turn).wait_send()
+        return carry
+
+    lax.fori_loop(1, devices, sent, 0)
 
     upper_rows, lower_rows = pl.ds(16, 32), pl.ds(0, 24)
     copies = []
@@ -401,13 +459,7 @@
 
 
 def per_device(part_cells, part_offsets, part_counts, w_first, w_mid, w_last, w_head, cotangent):
-    n_slab, n_sub = lax.axis_size("slab"), lax.axis_size("sub")
-    devices = n_slab * n_sub
-    slots = part_cells.shape[2]
-    live = jnp.arange(slots, dtype=jnp.int32)[None, :] < part_counts[0][:, None]
-    cells = jnp.where(live, part_cells[0], -1).astype(F32).reshape(devices, 2, 128)
-    packed = jnp.concatenate([cells, part_offsets[0].reshape(devices, 6, 128)], 1)
-    got = lax.all_to_all(packed, ("slab", "sub"), split_axis=0, concat_axis=0, tiled=True)
+    devices = part_counts.shape[1]
     vmem = pl.BlockSpec(memory_space=pltpu.VMEM)
     field = pltpu.VMEM((BY + 2, COLS, NZ), BF16)
     kept = pltpu.VMEM((BY, BX * CH, NZ), F32)
@@ -421,9 +473,11 @@
             jax.ShapeDtypeStruct(w_last.shape, F32),
             jax.ShapeDtypeStruct(w_head.shape, F32),
         ),
-        in_specs=[vmem] * 6,
+        in_specs=[vmem] * 8,
         out_specs=[vmem] * 5,
         scratch_shapes=[
+            pltpu.VMEM((devices * 8, 128), F32),
+            pltpu.VMEM((devices * 8, 128), F32),
             pltpu.VMEM((2, NZ, 256 * GROUP), BF16),
             pltpu.VMEM((2, 192, 256 * GROUP), BF16),
             pltpu.VMEM((48, NZ), F32),
@@ -448,12 +502,14 @@
             pltpu.SemaphoreType.DMA((5,)),
             pltpu.SemaphoreType.DMA((29,)),
             pltpu.SemaphoreType.DMA((29,)),
+            pltpu.SemaphoreType.DMA((devices,)),
+            pltpu.SemaphoreType.DMA((devices,)),
         ],
         compiler_params=pltpu.CompilerParams(
             collective_id=0, has_side_effects=True, vmem_limit_bytes=48 << 20
         ),
         name="level",
-    )(got, cotangent, w_first, w_mid, w_last, w_head)
+    )(part_cells, part_offsets, part_counts, cotangent, w_first, w_mid, w_last, w_head)
 
 
 def solution(mesh):

time: 92.7 us -> 84.5 us (0.912)
  blocking collectives: 25 us -> 0 us
  Pallas kernels: 60.3 us -> 79.3 us
  local copies, waits for them, and re-layouts: 6.07 us -> 4.38 us
    all_to_all x1 -> x0, blocking collectives: 25 us -> none  [per_device(): lax.all_to_all(packed, ('slab', 'sub'), split_axis=0, concat_axis=0, tile...]
    pallas_call x1, Pallas kernels: 60.3 us -> 79.3 us  [per_device(): pl.pallas_call(body, out_shape=(jax.ShapeDtypeStruct(cotangent.shape, BF1...]
    squeeze x1 -> x0, local copies, waits for them, and re-layouts: 0.97 us -> none  [per_device(): part_cells[0]]
    unnamed x18 -> x20, local copies, waits for them, and re-layouts: 4.86 us -> 4.38 us
where the time goes in v3:
time: 84.5 us; the launch traced here: 84.4 us
  Pallas kernels  79.3 us (94%)
  local copies, waits for them, and re-layouts  4.38 us (5%)
    pallas_call x1, Pallas kernels, per_device(): pl.pallas_call(body, out_shape=(jax.ShapeDtypeStruct(cotangent.shape, BF1...  79.3 us
    unnamed x20, local copies, waits for them, and re-layouts  4.38 us

profile of v3, /device:TPU:1, one launch (start us, length us, event | category | flops | bytes accessed | tf_op | source)
XLA Modules:
  0.0 84.4 jit_solution(10032016438776246168)
XLA Ops:
  0.6 0.0 copy-start.1
  0.6 0.0 copy-start.5
  0.7 0.0 copy-start.3
  0.7 0.0 copy-start.2
  0.7 0.0 copy-start.4
  0.7 0.0 copy-start.6
  0.7 0.0 copy-start
  0.7 1.3 %copy.13.offsets = f32[1,128,3,256]{3,2,1,0:T(4,128)S(1)} copy(f32[1,128,3,256]{3,1,2,0:T(8,128)} %param.9) | data formatting | bytes 786432 | tf_op args[1]
  2.0 0.0 copy-done.1
  2.0 0.0 copy-done.5
  2.1 0.0 copy-done.3
  2.1 0.0 copy-done.2
  2.1 0.0 copy-done.4
  2.1 0.0 copy-done.6
  2.1 0.0 copy-done
  2.1 79.3 %level.1 = (bf16[3,4,8,256]{3,2,1,0:T(8,128)(2,1)S(1)}, f32[16,27]{1,0:T(8,128)S(1)}, f32[16,432]{1,0:T(8,128)S(1)}, f32[16,432]{1,0:T(8,128)S(1)}, f32[3,32]{1,0:T(4,128)S(1)}) custom-call(s32[1,128,256]{2,1,0:T(8,128)S(1)} %copy-done, f32[1,128,3,256]{3,2,1,0:T(4,128)S(1)} %copy.13.offsets, s32[1,128]{1,0:T(1,128)S(1)} %copy-done.6, ...), custom_call_target="tpu_custom_call" | custom-call | tf_op jit(solution)/shard_map/level/pallas_call | solution.py:467
  81.4 0.6 copy.19
  82.0 0.6 copy.20
  82.6 0.6 copy.21
  83.2 0.6 copy.22
  83.8 0.6 copy.23
Async XLA Ops:
  0.6 1.4 %copy-start.1 = (bf16[3,4,8,256]{3,2,1,0:T(8,128)(2,1)S(1)}, bf16[3,4,8,256]{3,2,1,0:T(8,128)(2,1)}, u32[]{:S(2)}) copy-start(bf16[3,4,8,256]{3,2,1,0:T(8,128)(2,1)} %ct.1) | copy-start | bytes 147460
  0.6 1.4 %copy-start.5 = (bf16[3,32]{1,0:T(4,128)(2,1)S(1)}, bf16[3,32]{1,0:T(4,128)(2,1)}, u32[]{:S(2)}) copy-start(bf16[3,32]{1,0:T(4,128)(2,1)} %w_head_in.1) | copy-start | bytes 580
  0.7 1.4 %copy-start.3 = (bf16[16,432]{1,0:T(8,128)(2,1)S(1)}, bf16[16,432]{1,0:T(8,128)(2,1)}, u32[]{:S(2)}) copy-start(bf16[16,432]{1,0:T(8,128)(2,1)} %w_last_in.1) | copy-start | bytes 41476
  0.7 1.4 %copy-start.2 = (bf16[16,432]{1,0:T(8,128)(2,1)S(1)}, bf16[16,432]{1,0:T(8,128)(2,1)}, u32[]{:S(2)}) copy-start(bf16[16,432]{1,0:T(8,128)(2,1)} %w_mid_in.1) | copy-start | bytes 41476
  0.7 1.4 %copy-start.4 = (bf16[16,27]{1,0:T(8,128)(2,1)S(1)}, bf16[16,27]{1,0:T(8,128)(2,1)}, u32[]{:S(2)}) copy-start(bf16[16,27]{1,0:T(8,128)(2,1)} %w_first.1) | copy-start | bytes 2596
  0.7 1.4 %copy-start.6 = (s32[1,128]{1,0:T(1,128)S(1)}, s32[1,128]{1,0:T(1,128)}, u32[]{:S(2)}) copy-start(s32[1,128]{1,0:T(1,128)} %counts.1) | copy-start | bytes 1540
  0.7 1.4 %copy-start = (s32[1,128,256]{2,1,0:T(8,128)S(1)}, s32[1,128,256]{2,1,0:T(8,128)}, u32[]{:S(2)}) copy-start(s32[1,128,256]{2,1,0:T(8,128)} %cells.1) | copy-start | bytes 393220

commit v4 on v3

--- a/solution.py
+++ b/solution.py
@@ -16,7 +16,6 @@
 COLS = (BX + 2) * CH
 CORE = slice(CH, CH + BX * CH)
 GROUP = 4
-SPREAD = 1
 X_ROW = (0, 8, 24, 32, 40)
 
 
@@ -91,27 +90,41 @@
 
 
 def body(
-    cells, offsets, counts, ct, w_first, w_mid_in, w_last_in, w_head_in,
-    force, grad_first, grad_mid, grad_last, grad_head,
+    cells_hbm, offsets_hbm, counts, ct_hbm, w_first, w_mid_in, w_last_in, w_head_in,
+    force, sums,
+    cells, offsets, ct_own, ct_in, force_s,
     packed, got, hot_s, wt_s, dep, dep_in, dens_f, dens, one, two, g_three, g_two, pre_one, pre_two, acc,
-    base, w_one, w_mid, w_last, w_mid_t, w_last_t, head_f, head_b, ct_s, pay, half_in, ring, whole,
-    send, recv, send_d, recv_d, send_s, recv_s, send_p, recv_p,
+    base, w_one, w_mid, w_last, w_mid_t, w_last_t, head_f, head_b, ct_s,
+    pay, half_in, ring, tile, tile_in, tiles,
+    load, send, recv, send_d, recv_d, send_s, recv_s, send_p, recv_p, send_f, recv_f, send_m, recv_m,
 ):
     n_slab, n_sub = lax.axis_size("slab"), lax.axis_size("sub")
     slab, sub = lax.axis_index("slab"), lax.axis_index("sub")
-    up, down, other = (slab + 1) % n_slab, (slab + n_slab - 1) % n_slab, (sub + 1) % n_sub
-    neighbours = ((up, sub), (down, sub), (slab, other), (up, other), (down, other))
     devices = n_slab * n_sub
     me = slab * n_sub + sub
+    other = (sub + 1) % n_sub
+    stop = ring_stop(slab)
+    up, down = ring_slab((stop + 1) % n_slab), ring_slab((stop + n_slab - 1) % n_slab)
+    neighbours = ((up, sub), (down, sub), (slab, other), (up, other), (down, other))
+    worker, owner = (ring_slab(slab), other), (stop, other)
     axes = []
     for stride in (1, 4, 16):
         size = min(4, max(1, n_slab // stride))
         at = slab // stride % size
         axes.append((at, [slab + ((at + i) % size - at) * stride for i in range(1, size)]))
 
+    loads = [
+        pltpu.make_async_copy(src, dst, load.at[at])
+        for at, (src, dst) in enumerate(
+            ((cells_hbm.at[0], cells), (offsets_hbm.at[0], offsets), (ct_hbm, ct_own))
+        )
+    ]
+    for copy in loads:
+        copy.start()
+
     def partner(turn):
-        to = (me + turn * SPREAD) % devices
-        return (to // n_sub, to % n_sub), to
+        to = (me + turn) % devices
+        return (to // n_sub, to % n_sub), ring_stop(to // n_sub) * n_sub + (to + 1) % n_sub
 
     barrier = pltpu.get_barrier_semaphore()
 
@@ -120,6 +133,10 @@
         return carry
 
     lax.fori_loop(1, devices, greet, 0)
+    make_tables(w_first, w_mid_in, w_last_in, w_head_in, base, w_one, w_mid, w_last, w_mid_t,
+                w_last_t, head_f, head_b)
+    for copy in loads:
+        copy.wait()
 
     diagonal = lax.broadcasted_iota(jnp.int32, (devices, devices), 0) == lax.broadcasted_iota(
         jnp.int32, (devices, devices), 1
@@ -127,7 +144,7 @@
     used = jnp.broadcast_to(counts[...].astype(F32), (devices, devices))
     used = jnp.sum(jnp.where(diagonal, used, 0.0), 1, keepdims=True)
     slot = lax.broadcasted_iota(jnp.int32, (devices, 256), 1).astype(F32)
-    live = jnp.where(slot < used, cells[0].astype(F32), -1.0)
+    live = jnp.where(slot < used, cells[...].astype(F32), -1.0)
     for first in range(0, devices, 8):
         for half in range(2):
             rows = pl.ds(first * 8 + 4 * half + 3, 8, stride=8)
@@ -138,18 +155,10 @@
             to = step * 8 + k
             for half in range(2):
                 rows = pl.ds(to * 8 + 4 * half, 3)
-                packed[rows, :] = offsets[0, to, :, half * 128 : half * 128 + 128]
+                packed[rows, :] = offsets[to, :, half * 128 : half * 128 + 128]
         return carry
 
     lax.fori_loop(0, devices // 8, pack, 0)
-
-    make_tables(w_first, w_mid_in, w_last_in, w_head_in, base, w_one, w_mid, w_last, w_mid_t,
-                w_last_t, head_f, head_b)
-    ct_s[...] = jnp.zeros_like(ct_s)
-    for k in range(3):
-        for x in range(BX):
-            at = (k * BX + x) * BY
-            ct_s[at : at + BY] = ct[k, x]
 
     def remote(src, dst, at, device, sends, recvs):
         return pltpu.make_async_remote_copy(
@@ -162,30 +171,33 @@
     def tile_rows(at):
         return pl.ds(pl.multiple_of(at * 8, 8), 8)
 
-    def tile_copy(turn):
-        device, to = partner(turn)
-        return remote(
-            packed.at[tile_rows(to)], got.at[tile_rows(turn)], turn, device, send_p, recv_p
-        )
-
     def send_tile(turn, carry):
-        tile_copy(turn).start()
+        device, brick = partner(turn)
+        remote(
+            packed.at[tile_rows(brick)], got.at[tile_rows(turn)], turn // (2 * GROUP), device,
+            send_p, recv_p,
+        ).start()
         return carry
 
     lax.fori_loop(1, devices, send_tile, 0)
-    got[:8] = packed[tile_rows(me)]
-
-    def take(turn, carry):
-        tile_copy(turn).wait_recv()
-        return carry
+    got[:8] = packed[tile_rows(partner(0)[1])]
+    ct_copy = remote(ct_own, ct_in, 0, worker, send_f, recv_f)
+    ct_copy.start()
+
+    def arrived(step, tiles_in):
+        rows = pl.ds(0, tiles_in * 8)
+        return pltpu.make_async_copy(got.at[rows], got.at[rows], recv_p.at[step])
+
+    def left(step, tiles_out):
+        rows = pl.ds(0, tiles_out * 8)
+        return pltpu.make_async_copy(packed.at[rows], packed.at[rows], send_p.at[step])
 
     def gather(step, total):
-        lax.fori_loop(jnp.maximum(step * 2 * GROUP, 1), (step + 1) * 2 * GROUP, take, 0)
         for part in range(2):
             for k in range(GROUP):
-                tile = got[tile_rows(step * 2 * GROUP + part * GROUP + k)]
+                source = got[tile_rows(step * 2 * GROUP + part * GROUP + k)]
                 for half in range(2):
-                    hot, weights = source_terms(tile, half)
+                    hot, weights = source_terms(source, half)
                     at = k * 256 + half * 128
                     hot_s[part, :, at : at + 128] = hot
                     wt_s[part, :, at : at + 128] = weights
@@ -193,14 +205,21 @@
             total = total + result[:96] + result[96:]
         return total
 
-    dep2 = lax.fori_loop(0, devices // (2 * GROUP), gather, jnp.zeros((96, NZ), F32))
+    def wait_and_gather(step, total):
+        arrived(step, 2 * GROUP).wait()
+        return gather(step, total)
+
+    arrived(0, 2 * GROUP - 1).wait()
+    dep2 = gather(0, jnp.zeros((96, NZ), F32))
+    dep2 = lax.fori_loop(1, devices // (2 * GROUP), wait_and_gather, dep2)
     dep[...] = dep2[:48] + lane_roll(dep2[48:], 1)
-
-    def sent(turn, carry):
-        tile_copy(turn).wait_send()
+    left(0, 2 * GROUP - 1).wait()
+
+    def sent(step, carry):
+        left(step, 2 * GROUP).wait()
         return carry
 
-    lax.fori_loop(1, devices, sent, 0)
+    lax.fori_loop(1, devices // (2 * GROUP), sent, 0)
 
     upper_rows, lower_rows = pl.ds(16, 32), pl.ds(0, 24)
     copies = []
@@ -247,23 +266,24 @@
         if 1 <= y <= BY:
             pre_one[y - 1] = pre[CORE]
 
-    def rims(field, base):
-        right, left = pl.ds(BX * CH, CH), pl.ds(CH, CH)
-        before, after = pl.ds(0, CH), pl.ds((BX + 1) * CH, CH)
-        core, ys = pl.ds(CH, BX * CH), pl.ds(1, BY)
+    right, left_end = pl.ds(BX * CH, CH), pl.ds(CH, CH)
+    before, after = pl.ds(0, CH), pl.ds((BX + 1) * CH, CH)
+    core = pl.ds(CH, BX * CH)
+
+    def rims(field, base, part):
+        ys = pl.ds(1 + part * (BY // 2), BY // 2)
+        edge, to = (1, BY + 1) if part == 0 else (BY, 0)
         plan = (
+            ((slab, other), (edge, core), (to, core)),
+            ((up, other), (edge, right), (to, before)),
+            ((down, other), (edge, left_end), (to, after)),
             ((up, sub), (ys, right), (ys, before)),
-            ((down, sub), (ys, left), (ys, after)),
-            ((slab, other), (1, core), (BY + 1, core)),
-            ((slab, other), (BY, core), (0, core)),
-            ((up, other), (1, right), (BY + 1, before)),
-            ((up, other), (BY, right), (0, before)),
-            ((down, other), (1, left), (BY + 1, after)),
-            ((down, other), (BY, left), (0, after)),
+            ((down, sub), (ys, left_end), (ys, after)),
         )
         started = []
         for at, (device, src, dst) in enumerate(plan):
-            copy = remote(field.at[src], field.at[dst], base + at, device, send, recv)
+            place = base + part * len(plan) + at
+            copy = remote(field.at[src], field.at[dst], place, device, send, recv)
             copy.start()
             started.append(copy)
         return started
@@ -274,17 +294,27 @@
     def conv(taps, field, y):
         return join_z(dot(taps[...], planes(field, y)))
 
+    started = []
     for y in range(BY):
         pre = conv(w_mid, one, y)
         pre_two[y] = pre
         two[y + 1, CORE] = (pre * sigmoid(pre)).astype(BF16)
-    for copy in rims(two, 0):
+        if y % 4 == 3:
+            started += rims(two, 0, y // 4)
+    ct_copy.wait()
+    ct_s[...] = jnp.zeros_like(ct_s)
+    for k in range(3):
+        for x in range(BX):
+            at = (k * BX + x) * BY
+            ct_s[at : at + BY] = ct_in[k, x]
+    for copy in started:
         copy.wait()
 
     row_y = lax.broadcasted_iota(jnp.int32, (128, 128), 0) % BY
     lane_y = lax.broadcasted_iota(jnp.int32, (128, 128), 1) % BY
     out = jnp.zeros((96, NZ), F32)
     head = jnp.zeros((128, 128), F32)
+    started = []
     for y in range(BY):
         pre = conv(w_last, two, y)
         s = sigmoid(pre)
@@ -295,13 +325,16 @@
         taps = jnp.where(lane_y == y, head_b[...], 0.0)[: BX * CH].astype(BF16)
         back = dot(taps, ct_s[...])
         g_three[y + 1, CORE] = (back * (s * (1.0 + pre * (1.0 - s)))).astype(BF16)
-    started = rims(g_three, 8)
+        if y % 4 == 3:
+            started += rims(g_three, 10, y // 4)
     for k in range(3):
         for x in range(BX):
             at = (k * BX + x) * BY
-            force[k, x] = out[at : at + BY].astype(BF16)
-
-    def weight_grad(grads, field, shift):
+            force_s[k, x] = out[at : at + BY].astype(BF16)
+    force_copy = remote(force_s, force, 1, owner, send_f, recv_f)
+    force_copy.start()
+
+    def weight_grad(grads, field, out):
         acc[:, 3 * COLS :] = jnp.zeros((192, 96), F32)
         for y in range(BY):
             term = dot_nt(spread_z(grads[y + 1, CORE].astype(F32)), planes(field, y))
@@ -319,19 +352,102 @@
         joint = jnp.concatenate(rows, 0)
         lane = lax.broadcasted_iota(jnp.int32, joint.shape, 1)
         joint = jnp.where((lane % 96 < 48) & (lane < 3 * COLS), joint, 0.0)
-        return lane_roll(joint, shift) if shift else joint
-
-    sums = weight_grad(g_three, two, 48)
+        moved = [jnp.where(lane < 48, joint, 0.0)]
+        for dy in (1, 2):
+            inside = (lane >= 48 * dy) & (lane < 48 * dy + 48)
+            moved.append(jnp.where(inside, lane_roll(joint, -48 * dy), 0.0))
+        joint = moved[0] + moved[1] + moved[2]
+        out[:48] = joint[:, :128]
+        tail = joint[:CH, 128:256]
+        for dz in (1, 2):
+            tail = tail + lane_roll(joint[dz * CH : dz * CH + CH, 128:256], dz * CH)
+        out[48:] = tail
+
+    theirs = pl.ds(pl.multiple_of(other * 32, 8), 32)
+    mine = pl.ds(pl.multiple_of(sub * 32, 8), 32)
+
+    class Sum:
+        def __init__(self, at):
+            self.at, self.next, self.copies = at, at * 38, []
+
+        def begin(self, src, dst, device):
+            self.copies.append(remote(src, dst, self.next, device, send_s, recv_s))
+            self.copies[-1].start()
+            self.next += 1
+
+        def end(self):
+            for copy in self.copies:
+                copy.wait()
+            self.copies = []
+
+        def across(self):
+            self.begin(pay.at[self.at, theirs], half_in.at[self.at], (slab, other))
+
+        def joined(self):
+            self.end()
+            return pay[self.at, mine] + half_in[self.at]
+
+        def out(self, turn, total):
+            for part in range(4):
+                at, peers = axes[(part + turn) % 3]
+                rows = pl.ds(part * 8, 8)
+                ring[self.at, turn, at, rows] = total[part * 8 : part * 8 + 8]
+                for peer in peers:
+                    slot = ring.at[self.at, turn, at, rows]
+                    self.begin(slot, slot, (peer, sub))
+
+        def back(self, turn):
+            self.end()
+            parts = []
+            for part in range(4):
+                rows = slice(part * 8, part * 8 + 8)
+                value = ring[self.at, turn, 0, rows]
+                for slot in range(1, len(axes[(part + turn) % 3][1]) + 1):
+                    value = value + ring[self.at, turn, slot, rows]
+                parts.append(value)
+            return jnp.concatenate(parts, 0)
+
+        def share(self, total):
+            rows = pl.ds(pl.multiple_of(self.at * 64 + sub * 32, 8), 32)
+            sums[rows] = total * scale
+            self.begin(sums.at[rows], sums.at[rows], (slab, other))
+
+    scale = 1.0 / math.sqrt(BX * n_slab * BY * n_sub * NZ)
+    sum_last, sum_mid = Sum(0), Sum(1)
+
+    weight_grad(g_three, two, pay.at[0])
+    row = lax.broadcasted_iota(jnp.int32, (128, 128), 0)
+    lane = lax.broadcasted_iota(jnp.int32, (128, 128), 1)
+    head = jnp.where(lane % 64 // CH == row // BY % BX, head, 0.0)
+    kept = jnp.concatenate(
+        [jnp.sum(head[k * 32 : k * 32 + 32], 0, keepdims=True) for k in range(3)]
+        + [jnp.zeros((5, 128), F32)],
+        0,
+    )
+    kept = kept + lane_roll(kept, -2 * CH)
+    kept = kept + lane_roll(kept, -CH)
+    lane = lax.broadcasted_iota(jnp.int32, (8, 128), 1)
+    top = jnp.where(lane < CH, kept, 0.0) + jnp.where(
+        (lane >= CH) & (lane < 2 * CH), lane_roll(kept, -48), 0.0
+    )
+    pay[0, 48:56] += lane_roll(top, 48)
+    sum_last.across()
     for copy in started:
         copy.wait()
 
+    started = []
     for y in range(BY):
         back = conv(w_last_t, g_three, y)
         g_two[y + 1, CORE] = (back * slope(pre_two[y])).astype(BF16)
-    started = rims(g_two, 16)
-    sums = sums + weight_grad(g_two, one, 0)
+        if y % 4 == 3:
+            started += rims(g_two, 20, y // 4)
+    sum_last.out(0, sum_last.joined())
+    weight_grad(g_two, one, pay.at[1])
+    sum_mid.across()
+    sum_last.out(1, sum_last.back(0))
     for copy in started:
         copy.wait()
+    sum_mid.out(0, sum_mid.joined())
 
     first = jnp.zeros((192, 128), F32)
     for y in range(BY):
@@ -349,69 +465,63 @@
     joint = jnp.concatenate(rows, 0)
     lane = lax.broadcasted_iota(jnp.int32, joint.shape, 1)
     joint = jnp.where((lane % 16 < 3) & (lane < 48), joint, 0.0)
-    extra = lane_roll(joint, 32)
-    row = lax.broadcasted_iota(jnp.int32, (128, 128), 0)
-    lane = lax.broadcasted_iota(jnp.int32, (128, 128), 1)
-    head = jnp.where(lane % 64 // CH == row // BY % BX, head, 0.0)
-    kept = jnp.concatenate(
-        [jnp.sum(head[k * 32 : k * 32 + 32], 0, keepdims=True) for k in range(3)]
-        + [jnp.zeros((5, 128), F32)],
-        0,
-    )
-    kept = kept + lane_roll(kept, -2 * CH)
-    kept = kept + lane_roll(kept, -CH)
-    lane = lax.broadcasted_iota(jnp.int32, (8, 128), 1)
-    top = jnp.where(lane < CH, kept, 0.0) + jnp.where(
-        (lane >= CH) & (lane < 2 * CH), lane_roll(kept, -48), 0.0
-    )
-    top = lane_roll(top, 80)
-    pay[...] = sums
-    pay[:, 256:384] += extra
-    pay[:8, 256:384] += top
-
-    theirs = pl.ds(pl.multiple_of(other * 24, 8), 24)
-    mine = pl.ds(pl.multiple_of(sub * 24, 8), 24)
-    copy = remote(pay.at[theirs], half_in, 0, (slab, other), send_s, recv_s)
-    copy.start()
-    copy.wait()
-    total = pay[mine] + half_in[...]
-    at_sem = 1
-    for turn in range(3):
-        copies = []
-        for part in range(3):
-            at, peers = axes[(part + turn) % 3]
-            rows = pl.ds(part * 8, 8)
-            ring[turn, at, rows] = total[part * 8 : part * 8 + 8]
-            for peer in peers:
-                slot = ring.at[turn, at, rows]
-                copies.append(remote(slot, slot, at_sem, (peer, sub), send_s, recv_s))
-                copies[-1].start()
-                at_sem += 1
-        for copy in copies:
-            copy.wait()
-        parts = []
-        for part in range(3):
-            size = len(axes[(part + turn) % 3][1]) + 1
-            rows = slice(part * 8, part * 8 + 8)
-            value = ring[turn, 0, rows]
-            for slot in range(1, size):
-                value = value + ring[turn, slot, rows]
-            parts.append(value)
-        total = jnp.concatenate(parts, 0)
-    whole[mine] = total * (1.0 / math.sqrt(BX * n_slab * BY * n_sub * NZ))
-    copy = remote(whole.at[mine], whole.at[mine], at_sem, (slab, other), send_s, recv_s)
-    copy.start()
-    copy.wait()
+    value = jnp.zeros((8, 128), F32)
+    for block, shift in enumerate(BLOCK_LANE):
+        value = value + lane_roll(joint[block * 8 : block * 8 + 8], shift)
+    tile[...] = value
+    tile_copy = remote(tile, tile_in, 2, (slab, other), send_f, recv_f)
+    tile_copy.start()
+    sum_mid.out(1, sum_mid.back(0))
+    sum_last.out(2, sum_last.back(1))
+    tile_copy.wait()
+    tiles[slab] = tile[...] + tile_in[...]
+    if n_slab > 1:
+
+        def spread_tile(turn, carry):
+            peer = (slab + 1 + (turn + n_slab * 2 // 3) % (n_slab - 1)) % n_slab
+            remote(tiles.at[slab], tiles.at[slab], 0, (peer, sub), send_m, recv_m).start()
+            return carry
+
+        lax.fori_loop(0, n_slab - 1, spread_tile, 0)
+    sum_mid.out(2, sum_mid.back(1))
+    sum_last.share(sum_last.back(2))
+    sum_mid.share(sum_mid.back(2))
+    if n_slab > 1:
+        some = pl.ds(0, n_slab - 1)
+        pltpu.make_async_copy(tiles.at[some], tiles.at[some], recv_m.at[0]).wait()
+        pltpu.make_async_copy(tiles.at[some], tiles.at[some], send_m.at[0]).wait()
+    sums[128:136] = jnp.sum(tiles[...], 0) * scale
+    sum_last.end()
+    sum_mid.end()
+    force_copy.wait()
+
+
+def ring_stop(slab):
+    y = (slab // 4 + slab // 16) % 4
+    return slab // 16 * 16 + y * 4 + (slab + y) % 4
+
+
+def ring_slab(stop):
+    z, y = stop // 16, stop // 4 % 4
+    return z * 16 + (y + 4 - z) % 4 * 4 + (stop + 4 - y) % 4
+
+
+def finish(force_in, sums, force, grad_first, grad_mid, grad_last, grad_head):
+    force[...] = force_in[...]
     for dx, dy, dz in OFFSETS:
-        rows, tap = slice(dz * CH, dz * CH + CH), dx * 9 + dy * 3 + dz
-        at, to = dy * 96 + dx * CH, slice(tap * CH, tap * CH + CH)
-        grad_mid[:, to] = whole[rows, at : at + CH]
-        grad_last[:, to] = whole[rows, at + 48 : at + 48 + CH]
-        at = 288 + dx * CH + dy
-        grad_first[:, tap : tap + 1] = whole[rows, at : at + 1]
-    grad_head[...] = whole[:3, 336:368]
-
-
+        tap, rows, at = dx * 9 + dy * 3 + dz, dz * CH, dy * 48 + dx * CH
+        if at == 128:
+            rows, at = 48, dz * CH
+        for first, out in ((64, grad_mid), (0, grad_last)):
+            block = sums[first + rows : first + rows + CH, at : at + CH]
+            out[:, tap * CH : tap * CH + CH] = block
+        for half in range(2):
+            at = BLOCK_LANE[2 * dz + half] + dx * CH + dy
+            grad_first[half * 8 : half * 8 + 8, tap : tap + 1] = sums[128:136, at : at + 1]
+    grad_head[...] = sums[48:51, 48:80]
+
+
+BLOCK_LANE = (0, 3, 6, 9, 12, 48)
 OFFSETS = [(dx, dy, dz) for dx in range(3) for dy in range(3) for dz in range(3)]
 
 
@@ -464,18 +574,22 @@
     field = pltpu.VMEM((BY + 2, COLS, NZ), BF16)
     kept = pltpu.VMEM((BY, BX * CH, NZ), F32)
     table = pltpu.VMEM((192, 3 * COLS), BF16)
-    return pl.pallas_call(
+    hbm = pl.BlockSpec(memory_space=pltpu.HBM)
+    slots = part_cells.shape[2]
+    force, sums = pl.pallas_call(
         body,
         out_shape=(
             jax.ShapeDtypeStruct(cotangent.shape, BF16),
-            jax.ShapeDtypeStruct(w_first.shape, F32),
-            jax.ShapeDtypeStruct(w_mid.shape, F32),
-            jax.ShapeDtypeStruct(w_last.shape, F32),
-            jax.ShapeDtypeStruct(w_head.shape, F32),
+            jax.ShapeDtypeStruct((136, 128), F32),
         ),
-        in_specs=[vmem] * 8,
-        out_specs=[vmem] * 5,
+        in_specs=[hbm, hbm, vmem, hbm, vmem, vmem, vmem, vmem],
+        out_specs=[vmem] * 2,
         scratch_shapes=[
+            pltpu.VMEM((devices, slots), jnp.int32),
+            pltpu.VMEM((devices, 3, slots), F32),
+            pltpu.VMEM(cotangent.shape, BF16),
+            pltpu.VMEM(cotangent.shape, BF16),
+            pltpu.VMEM(cotangent.shape, BF16),
             pltpu.VMEM((devices * 8, 128), F32),
             pltpu.VMEM((devices * 8, 128), F32),
             pltpu.VMEM((2, NZ, 256 * GROUP), BF16),
@@ -492,24 +606,44 @@
             pltpu.VMEM((128, 128), F32),
             pltpu.VMEM((128, 128), F32),
             pltpu.VMEM((128, NZ), BF16),
-            pltpu.VMEM((48, 384), F32),
-            pltpu.VMEM((24, 384), F32),
-            pltpu.VMEM((3, 4, 24, 384), F32),
-            pltpu.VMEM((48, 384), F32),
-            pltpu.SemaphoreType.DMA((24,)),
-            pltpu.SemaphoreType.DMA((24,)),
+            pltpu.VMEM((2, 64, 128), F32),
+            pltpu.VMEM((2, 32, 128), F32),
+            pltpu.VMEM((2, 3, 4, 32, 128), F32),
+            pltpu.VMEM((8, 128), F32),
+            pltpu.VMEM((8, 128), F32),
+            pltpu.VMEM((devices // 2, 8, 128), F32),
+            pltpu.SemaphoreType.DMA((3,)),
+            pltpu.SemaphoreType.DMA((30,)),
+            pltpu.SemaphoreType.DMA((30,)),
             pltpu.SemaphoreType.DMA((5,)),
             pltpu.SemaphoreType.DMA((5,)),
-            pltpu.SemaphoreType.DMA((29,)),
-            pltpu.SemaphoreType.DMA((29,)),
-            pltpu.SemaphoreType.DMA((devices,)),
-            pltpu.SemaphoreType.DMA((devices,)),
+            pltpu.SemaphoreType.DMA((76,)),
+            pltpu.SemaphoreType.DMA((76,)),
+            pltpu.SemaphoreType.DMA((devices // (2 * GROUP),)),
+            pltpu.SemaphoreType.DMA((devices // (2 * GROUP),)),
+            pltpu.SemaphoreType.DMA((3,)),
+            pltpu.SemaphoreType.DMA((3,)),
+            pltpu.SemaphoreType.DMA((1,)),
+            pltpu.SemaphoreType.DMA((1,)),
         ],
         compiler_params=pltpu.CompilerParams(
             collective_id=0, has_side_effects=True, vmem_limit_bytes=48 << 20
         ),
         name="level",
     )(part_cells, part_offsets, part_counts, cotangent, w_first, w_mid, w_last, w_head)
+    return pl.pallas_call(
+        finish,
+        out_shape=(
+            jax.ShapeDtypeStruct(cotangent.shape, BF16),
+            jax.ShapeDtypeStruct(w_first.shape, F32),
+            jax.ShapeDtypeStruct(w_mid.shape, F32),
+            jax.ShapeDtypeStruct(w_last.shape, F32),
+            jax.ShapeDtypeStruct(w_head.shape, F32),
+        ),
+        in_specs=[vmem] * 2,
+        out_specs=[vmem] * 5,
+        name="finish",
+    )(force, sums)
 
 
 def solution(mesh):

time: 84.5 us -> 71.4 us (0.84)
  Pallas kernels: 79.3 us -> 67.9 us
  local copies, waits for them, and re-layouts: 4.38 us -> 2.58 us
    pallas_call x1, Pallas kernels: 79.3 us -> 66.1 us  [per_device(): pl.pallas_call(body, out_shape=(jax.ShapeDtypeStruct(cotangent.shape, BF1...]
    unnamed x20 -> x19, local copies, waits for them, and re-layouts: 4.38 us -> 2.58 us
    pallas_call x0 -> x1, Pallas kernels: none -> 1.73 us  [per_device(): pl.pallas_call(finish, out_shape=(jax.ShapeDtypeStruct(cotangent.shape, B...]
where the time goes in v4:
time: 71.4 us; the launch traced here: 71.2 us
  Pallas kernels  67.9 us (95%)
  local copies, waits for them, and re-layouts  2.58 us (4%)
  between operations  0.76 us (1%)
    pallas_call x1, Pallas kernels, per_device(): pl.pallas_call(body, out_shape=(jax.ShapeDtypeStruct(cotangent.shape, BF1...  66.1 us
    unnamed x19, local copies, waits for them, and re-layouts  2.58 us
    pallas_call x1, Pallas kernels, per_device(): pl.pallas_call(finish, out_shape=(jax.ShapeDtypeStruct(cotangent.shape, B...  1.73 us

profile of v4, /device:TPU:1, one launch (start us, length us, event | category | flops | bytes accessed | tf_op | source)
XLA Modules:
  0.0 71.2 jit_solution(14853967358913242648)
XLA Ops:
  0.6 0.0 copy-start.2
  0.6 0.0 copy-start.7
  0.7 0.0 copy-start.5
  0.7 0.0 copy-start.4
  0.7 0.0 copy-start.6
  0.7 0.0 copy-start.8
  0.7 0.0 copy-start
  0.7 1.3 %copy.13.offsets_hbm = f32[1,128,3,256]{3,2,1,0:T(4,128)S(1)} copy(f32[1,128,3,256]{3,1,2,0:T(8,128)} %param.9) | data formatting | bytes 786432 | tf_op args[1]
  2.0 0.0 copy-done.2
  2.0 0.0 copy-done.7
  2.1 0.0 copy-done.5
  2.1 0.0 copy-done.4
  2.1 0.0 copy-done.6
  2.1 0.0 copy-done.8
  2.1 0.0 copy-done
  2.1 66.1 %level.1 = (bf16[3,4,8,256]{3,2,1,0:T(8,128)(2,1)S(1)}, f32[136,128]{1,0:T(8,128)S(1)}) custom-call(s32[1,128,256]{2,1,0:T(8,128)S(1)} %copy-done, f32[1,128,3,256]{3,2,1,0:T(4,128)S(1)} %copy.13.offsets_hbm, s32[1,128]{1,0:T(1,128)S(1)} %copy-done.8, bf16[3,4,8,256]{3,2,1,0:T(8,128)(2,1)S(1)} %copy-done.2, bf16[16,27]{1,0:T(8,128)(2,1)S(1)} %copy-done.6, ...), custom_call_target="tpu_custom_call" | custom-call | tf_op jit(solution)/shard_map/level/pallas_call | solution.py:579
  68.2 0.0 copy-start.1
  68.2 0.6 copy-done.1
  68.8 0.0 copy-start.3
  68.9 0.6 copy-done.3
  69.5 1.7 %finish.1 = (bf16[3,4,8,256]{3,2,1,0:T(8,128)(2,1)}, f32[16,27]{1,0:T(8,128)}, f32[16,432]{1,0:T(8,128)}, f32[16,432]{1,0:T(8,128)}, f32[3,32]{1,0:T(4,128)}) custom-call(bf16[3,4,8,256]{3,2,1,0:T(8,128)(2,1)} %copy-done.3, f32[136,128]{1,0:T(8,128)} %copy-done.1), custom_call_target="tpu_custom_call" | custom-call | tf_op jit(solution)/shard_map/finish/pallas_call | solution.py:634
Async XLA Ops:
  0.6 1.4 %copy-start.2 = (bf16[3,4,8,256]{3,2,1,0:T(8,128)(2,1)S(1)}, bf16[3,4,8,256]{3,2,1,0:T(8,128)(2,1)}, u32[]{:S(2)}) copy-start(bf16[3,4,8,256]{3,2,1,0:T(8,128)(2,1)} %ct_hbm.1) | copy-start | bytes 147460
  0.6 1.4 %copy-start.7 = (bf16[3,32]{1,0:T(4,128)(2,1)S(1)}, bf16[3,32]{1,0:T(4,128)(2,1)}, u32[]{:S(2)}) copy-start(bf16[3,32]{1,0:T(4,128)(2,1)} %w_head_in.1) | copy-start | bytes 580
  0.7 1.4 %copy-start.5 = (bf16[16,432]{1,0:T(8,128)(2,1)S(1)}, bf16[16,432]{1,0:T(8,128)(2,1)}, u32[]{:S(2)}) copy-start(bf16[16,432]{1,0:T(8,128)(2,1)} %w_last_in.1) | copy-start | bytes 41476
  0.7 1.4 %copy-start.4 = (bf16[16,432]{1,0:T(8,128)(2,1)S(1)}, bf16[16,432]{1,0:T(8,128)(2,1)}, u32[]{:S(2)}) copy-start(bf16[16,432]{1,0:T(8,128)(2,1)} %w_mid_in.1) | copy-start | bytes 41476
  0.7 1.4 %copy-start.6 = (bf16[16,27]{1,0:T(8,128)(2,1)S(1)}, bf16[16,27]{1,0:T(8,128)(2,1)}, u32[]{:S(2)}) copy-start(bf16[16,27]{1,0:T(8,128)(2,1)} %w_first.1) | copy-start | bytes 2596
  0.7 1.4 %copy-start.8 = (s32[1,128]{1,0:T(1,128)S(1)}, s32[1,128]{1,0:T(1,128)}, u32[]{:S(2)}) copy-start(s32[1,128]{1,0:T(1,128)} %counts.1) | copy-start | bytes 1540
  0.7 1.4 %copy-start = (s32[1,128,256]{2,1,0:T(8,128)S(1)}, s32[1,128,256]{2,1,0:T(8,128)}, u32[]{:S(2)}) copy-start(s32[1,128,256]{2,1,0:T(8,128)} %cells_hbm.1) | copy-start | bytes 393220
  68.2 0.6 copy-start.1
  68.8 0.6 copy-start.3

commit v5 on v4

--- a/solution.py
+++ b/solution.py
@@ -146,19 +146,12 @@
     slot = lax.broadcasted_iota(jnp.int32, (devices, 256), 1).astype(F32)
     live = jnp.where(slot < used, cells[...].astype(F32), -1.0)
     for first in range(0, devices, 8):
+        some = slice(first, first + 8)
         for half in range(2):
-            rows = pl.ds(first * 8 + 4 * half + 3, 8, stride=8)
-            packed[rows, :] = live[first : first + 8, half * 128 : half * 128 + 128]
-
-    def pack(step, carry):
-        for k in range(8):
-            to = step * 8 + k
-            for half in range(2):
-                rows = pl.ds(to * 8 + 4 * half, 3)
-                packed[rows, :] = offsets[to, :, half * 128 : half * 128 + 128]
-        return carry
-
-    lax.fori_loop(0, devices // 8, pack, 0)
+            lanes = slice(half * 128, half * 128 + 128)
+            for part in range(4):
+                rows = pl.ds(first * 8 + 4 * half + part, 8, stride=8)
+                packed[rows, :] = offsets[part, some, lanes] if part < 3 else live[some, lanes]
 
     def remote(src, dst, at, device, sends, recvs):
         return pltpu.make_async_remote_copy(
@@ -586,7 +579,7 @@
         out_specs=[vmem] * 2,
         scratch_shapes=[
             pltpu.VMEM((devices, slots), jnp.int32),
-            pltpu.VMEM((devices, 3, slots), F32),
+            pltpu.VMEM((3, devices, slots), F32),
             pltpu.VMEM(cotangent.shape, BF16),
             pltpu.VMEM(cotangent.shape, BF16),
             pltpu.VMEM(cotangent.shape, BF16),
@@ -627,10 +620,10 @@
             pltpu.SemaphoreType.DMA((1,)),
         ],
         compiler_params=pltpu.CompilerParams(
-            collective_id=0, has_side_effects=True, vmem_limit_bytes=48 << 20
+            collective_id=0, has_side_effects=True, vmem_limit_bytes=60 << 20
         ),
         name="level",
-    )(part_cells, part_offsets, part_counts, cotangent, w_first, w_mid, w_last, w_head)
+    )(part_cells, part_offsets.transpose(0, 2, 1, 3), part_counts, cotangent, w_first, w_mid, w_last, w_head)
     return pl.pallas_call(
         finish,
         out_shape=(
@@ -642,6 +635,7 @@
         ),
         in_specs=[vmem] * 2,
         out_specs=[vmem] * 5,
+        compiler_params=pltpu.CompilerParams(vmem_limit_bytes=60 << 20),
         name="finish",
     )(force, sums)
 

time: 71.4 us -> 69.3 us (0.971)
  local copies, waits for them, and re-layouts: 2.58 us -> 0 us
    unnamed x19 -> x0, local copies, waits for them, and re-layouts: 2.58 us -> none
where the time goes in v5:
time: 69.3 us; the launch traced here: 69.1 us
  Pallas kernels  68.5 us (99%)
    pallas_call x1, Pallas kernels, per_device(): pl.pallas_call(body, out_shape=(jax.ShapeDtypeStruct(cotangent.shape, BF1...  66.7 us
    pallas_call x1, Pallas kernels, per_device(): pl.pallas_call(finish, out_shape=(jax.ShapeDtypeStruct(cotangent.shape, B...  1.74 us

profile of v5, /device:TPU:1, one launch (start us, length us, event | category | flops | bytes accessed | tf_op | source)
XLA Modules:
  0.0 69.1 jit_solution(1726911801788158518)
XLA Ops:
  0.6 66.7 %level.1 = (bf16[3,4,8,256]{3,2,1,0:T(8,128)(2,1)}, f32[136,128]{1,0:T(8,128)}) custom-call(s32[1,128,256]{2,1,0:T(8,128)} %cells_hbm.1, f32[1,3,128,256]{3,2,1,0:T(8,128)} %bitcast.1, s32[1,128]{1,0:T(1,128)} %counts.1, bf16[3,4,8,256]{3,2,1,0:T(8,128)(2,1)} %ct_hbm.1, bf16[16,27]{1,0:T(8,128)(2,1)} %w_first.1, bf16[16,432]{1,0:T(8,128)(2,1)} %w_mid_in.1, ...), custom_call_target="tpu_custom_call" | custom-call | tf_op jit(solution)/shard_map/level/pallas_call | solution.py:572
  67.4 1.7 %finish.1 = (bf16[3,4,8,256]{3,2,1,0:T(8,128)(2,1)}, f32[16,27]{1,0:T(8,128)}, f32[16,432]{1,0:T(8,128)}, f32[16,432]{1,0:T(8,128)}, f32[3,32]{1,0:T(4,128)}) custom-call(bf16[3,4,8,256]{3,2,1,0:T(8,128)(2,1)} %get-tuple-element.7.force_in, f32[136,128]{1,0:T(8,128)} %get-tuple-element.8.sums), custom_call_target="tpu_custom_call" | custom-call | tf_op jit(solution)/shard_map/finish/pallas_call | solution.py:627

commit v6 on v5

--- a/solution.py
+++ b/solution.py
@@ -185,26 +185,34 @@
         rows = pl.ds(0, tiles_out * 8)
         return pltpu.make_async_copy(packed.at[rows], packed.at[rows], send_p.at[step])
 
+    def build(step, part):
+        for k in range(GROUP):
+            source = got[tile_rows(step * 2 * GROUP + part * GROUP + k)]
+            for half in range(2):
+                hot, weights = source_terms(source, half)
+                at = k * 256 + half * 128
+                hot_s[part, :, at : at + 128] = hot
+                wt_s[part, :, at : at + 128] = weights
+
+    def product(part):
+        result = dot_nt(wt_s[part], hot_s[part])
+        return result[:96] + result[96:]
+
     def gather(step, total):
-        for part in range(2):
-            for k in range(GROUP):
-                source = got[tile_rows(step * 2 * GROUP + part * GROUP + k)]
-                for half in range(2):
-                    hot, weights = source_terms(source, half)
-                    at = k * 256 + half * 128
-                    hot_s[part, :, at : at + 128] = hot
-                    wt_s[part, :, at : at + 128] = weights
-            result = dot_nt(wt_s[part], hot_s[part])
-            total = total + result[:96] + result[96:]
+        total = total + product(0)
+        build(step, 1)
+        arrived(step + 1, 2 * GROUP).wait()
+        total = total + product(1)
+        build(step + 1, 0)
         return total
 
-    def wait_and_gather(step, total):
-        arrived(step, 2 * GROUP).wait()
-        return gather(step, total)
-
+    steps = devices // (2 * GROUP)
     arrived(0, 2 * GROUP - 1).wait()
-    dep2 = gather(0, jnp.zeros((96, NZ), F32))
-    dep2 = lax.fori_loop(1, devices // (2 * GROUP), wait_and_gather, dep2)
+    build(0, 0)
+    dep2 = lax.fori_loop(0, steps - 1, gather, jnp.zeros((96, NZ), F32))
+    dep2 = dep2 + product(0)
+    build(steps - 1, 1)
+    dep2 = dep2 + product(1)
     dep[...] = dep2[:48] + lane_roll(dep2[48:], 1)
     left(0, 2 * GROUP - 1).wait()
 

time: 69.3 us -> 77.5 us (1.12)
  Pallas kernels: 68.5 us -> 76.6 us
    pallas_call x1, Pallas kernels: 66.7 us -> 74.9 us  [per_device(): pl.pallas_call(body, out_shape=(jax.ShapeDtypeStruct(cotangent.shape, BF1...]
where the time goes in v6:
time: 77.5 us; the launch traced here: 77.3 us
  Pallas kernels  76.6 us (99%)
    pallas_call x1, Pallas kernels, per_device(): pl.pallas_call(body, out_shape=(jax.ShapeDtypeStruct(cotangent.shape, BF1...  74.9 us
    pallas_call x1, Pallas kernels, per_device(): pl.pallas_call(finish, out_shape=(jax.ShapeDtypeStruct(cotangent.shape, B...  1.74 us

profile of v6, /device:TPU:1, one launch (start us, length us, event | category | flops | bytes accessed | tf_op | source)
XLA Modules:
  0.0 77.3 jit_solution(16272936852411302064)
XLA Ops:
  0.6 74.9 %level.1 = (bf16[3,4,8,256]{3,2,1,0:T(8,128)(2,1)}, f32[136,128]{1,0:T(8,128)}) custom-call(s32[1,128,256]{2,1,0:T(8,128)} %cells_hbm.1, f32[1,3,128,256]{3,2,1,0:T(8,128)} %bitcast.1, s32[1,128]{1,0:T(1,128)} %counts.1, bf16[3,4,8,256]{3,2,1,0:T(8,128)(2,1)} %ct_hbm.1, bf16[16,27]{1,0:T(8,128)(2,1)} %w_first.1, bf16[16,432]{1,0:T(8,128)(2,1)} %w_mid_in.1, ...), custom_call_target="tpu_custom_call" | custom-call | tf_op jit(solution)/shard_map/level/pallas_call | solution.py:580
  75.5 1.7 %finish.1 = (bf16[3,4,8,256]{3,2,1,0:T(8,128)(2,1)}, f32[16,27]{1,0:T(8,128)}, f32[16,432]{1,0:T(8,128)}, f32[16,432]{1,0:T(8,128)}, f32[3,32]{1,0:T(4,128)}) custom-call(bf16[3,4,8,256]{3,2,1,0:T(8,128)(2,1)} %get-tuple-element.7.force_in, f32[136,128]{1,0:T(8,128)} %get-tuple-element.8.sums), custom_call_target="tpu_custom_call" | custom-call | tf_op jit(solution)/shard_map/finish/pallas_call | solution.py:635

commit v7 on v5

--- a/solution.py
+++ b/solution.py
@@ -174,8 +174,6 @@
 
     lax.fori_loop(1, devices, send_tile, 0)
     got[:8] = packed[tile_rows(partner(0)[1])]
-    ct_copy = remote(ct_own, ct_in, 0, worker, send_f, recv_f)
-    ct_copy.start()
 
     def arrived(step, tiles_in):
         rows = pl.ds(0, tiles_in * 8)
@@ -206,13 +204,6 @@
     dep2 = gather(0, jnp.zeros((96, NZ), F32))
     dep2 = lax.fori_loop(1, devices // (2 * GROUP), wait_and_gather, dep2)
     dep[...] = dep2[:48] + lane_roll(dep2[48:], 1)
-    left(0, 2 * GROUP - 1).wait()
-
-    def sent(step, carry):
-        left(step, 2 * GROUP).wait()
-        return carry
-
-    lax.fori_loop(1, devices // (2 * GROUP), sent, 0)
 
     upper_rows, lower_rows = pl.ds(16, 32), pl.ds(0, 24)
     copies = []
@@ -236,8 +227,17 @@
         dens_f[base + 2 : base + 3] += source[16 + source_x : 17 + source_x]
         dens_f[base + 10 : base + 12] += source[row : row + 2]
 
+    ct_copy = remote(ct_own, ct_in, 0, worker, send_f, recv_f)
+    ct_copy.start()
     for x in range(BX + 1):
         place(dep, x, x)
+    left(0, 2 * GROUP - 1).wait()
+
+    def sent(step, carry):
+        left(step, 2 * GROUP).wait()
+        return carry
+
+    lax.fori_loop(1, devices // (2 * GROUP), sent, 0)
     for copy in copies:
         copy.wait()
     for x in (2, 3, 4):

time: 69.3 us -> 69.1 us (level)
  no operation moved by 1% of the time
where the time goes in v7:
time: 69.1 us; the launch traced here: 68.9 us
  Pallas kernels  68.3 us (99%)
    pallas_call x1, Pallas kernels, per_device(): pl.pallas_call(body, out_shape=(jax.ShapeDtypeStruct(cotangent.shape, BF1...  66.6 us
    pallas_call x1, Pallas kernels, per_device(): pl.pallas_call(finish, out_shape=(jax.ShapeDtypeStruct(cotangent.shape, B...  1.74 us

profile of v7, /device:TPU:1, one launch (start us, length us, event | category | flops | bytes accessed | tf_op | source)
XLA Modules:
  0.0 68.9 jit_solution(15974334117689680198)
XLA Ops:
  0.6 66.6 %level.1 = (bf16[3,4,8,256]{3,2,1,0:T(8,128)(2,1)}, f32[136,128]{1,0:T(8,128)}) custom-call(s32[1,128,256]{2,1,0:T(8,128)} %cells_hbm.1, f32[1,3,128,256]{3,2,1,0:T(8,128)} %bitcast.1, s32[1,128]{1,0:T(1,128)} %counts.1, bf16[3,4,8,256]{3,2,1,0:T(8,128)(2,1)} %ct_hbm.1, bf16[16,27]{1,0:T(8,128)(2,1)} %w_first.1, bf16[16,432]{1,0:T(8,128)(2,1)} %w_mid_in.1, ...), custom_call_target="tpu_custom_call" | custom-call | tf_op jit(solution)/shard_map/level/pallas_call | solution.py:572
  67.2 1.7 %finish.1 = (bf16[3,4,8,256]{3,2,1,0:T(8,128)(2,1)}, f32[16,27]{1,0:T(8,128)}, f32[16,432]{1,0:T(8,128)}, f32[16,432]{1,0:T(8,128)}, f32[3,32]{1,0:T(4,128)}) custom-call(bf16[3,4,8,256]{3,2,1,0:T(8,128)(2,1)} %get-tuple-element.7.force_in, f32[136,128]{1,0:T(8,128)} %get-tuple-element.8.sums), custom_call_target="tpu_custom_call" | custom-call | tf_op jit(solution)/shard_map/finish/pallas_call | solution.py:627
